TPU v7x, 128 devices: a whole 4x4x4 slice. The times are simulated.
128 devices in a mesh: front: 4 (over x), row: 4 (over y), col: 8 (over z, core).
Axes of the slice: x: 4, y: 4, z: 4, core: 2. Of those that a mesh axis runs over, the one named last changes fastest.
Arguments:
- front_in: float32 [32768, 8192], P(('front', 'row'), 'col'), parts along dimension 0, may hold values from -6 to 6
- child_tiles: bfloat16 [128, 224, 128, 128], P(('front', 'row', 'col')), parts along dimension 0, may hold values from -6 to 6
- child_map: int32 [128, 224], P(('front', 'row', 'col')), parts along dimension 0, may hold values from 0 to 4095, as said below
- pattern: int32 [256, 64], P('front'), parts along dimension 0, may hold values 0 or 1
- pivot_inverse: float32 [8, 512, 512], P('front'), parts along dimension 0, may hold values from -0.01171875 to 0.01171875
Outputs:
- front_out: float32 [32768, 8192], P(('front', 'row'), 'col'), parts along dimension 0
There are 4 independent parts, one for each index of `front`. A program takes and returns all parts, laid end to end along the dimension named above; each array names one. Nothing has to cross between parts.
Inputs may be any that keep to these rules, and one draw needn't show every extreme that they name: Entries j * 7 to (j + 1) * 7 - 1 of each row of child_map name tiles held by device j of the front's grid, j = grid row * 8 + grid column, that device holding tile rows of its 2048 rows and tile columns of its 1024 columns.
All inputs are finite; a program needn't handle non-finite values.
Results may differ from a plain program's by a relative error of at most 0.0062.
Values may be sent and summed in bfloat16 or wider, within the bound.
A program may use at most 128 MiB of HBM per device.

v0:
```python
import jax
import jax.numpy as jnp
from jax import lax
from jax.sharding import Mesh
from jax.sharding import PartitionSpec as P

TILE = 128
PANEL = 512
PANELS = 2
SLOTS = 7
NT = 64
COL = ("col_0", "col_1")
ROW_COL = ("row", "col_0", "col_1")
FRONT_ROW_COL = ("front", "row", "col_0", "col_1")


def from_root(x, axes, root):
    x = jnp.where(lax.axis_index(axes) == root, x, jnp.zeros_like(x))
    for axis in axes:
        x = lax.psum(x, axis)
    return x


def cut_along(x, dim, count):
    shape = x.shape
    pieces = x.reshape(*shape[:dim], count, shape[dim] // count, *shape[dim + 1 :])
    return jnp.moveaxis(pieces, dim, 0)


def edges_of(length, count):
    lap = length // count
    if lap >= 8:
        lap -= lap % 8
    return [lap * k for k in range(1, count)]


def laid_out(pieces, dim):
    pieces = jnp.moveaxis(pieces, 0, dim)
    shape = pieces.shape
    return pieces.reshape(*shape[:dim], shape[dim] * shape[dim + 1], *shape[dim + 2 :])


def cut_exchange(x, axis, pieces, split_dim, concat_dim):
    blocks = cut_along(x, split_dim, lax.axis_size(axis))
    cut = max(range(1, max(2, blocks.ndim - 1)), key=lambda d: blocks.shape[d])
    gathered = []
    for piece in jnp.split(blocks, edges_of(blocks.shape[cut], pieces), axis=cut):
        if piece.size:
            gathered.append(lax.all_to_all(piece, axis, split_axis=0, concat_axis=0, tiled=True))
    return laid_out(jnp.concatenate(gathered, axis=cut), concat_dim)


def padded_to(lines, count):
    spare = -lines.shape[0] % count
    if not spare:
        return lines
    return jnp.concatenate([lines, jnp.zeros((spare, *lines.shape[1:]), lines.dtype)])


def spread(x, axis, root):
    lines = jnp.where(lax.axis_index(axis) == root, x, jnp.zeros_like(x)).reshape(
        -1, *x.shape[1:][-1:]
    )
    padded = padded_to(lines, lax.axis_size(axis))
    own = lax.psum_scatter(padded, axis, scatter_dimension=0, tiled=True)
    return lax.all_gather(own, axis, axis=0, tiled=True)[: len(lines)].reshape(x.shape)


def factor_panel(matrix, inverse, panel_index):
    first_col = panel_index * PANEL
    lower_part = jnp.dot(
        matrix[:, first_col : first_col + PANEL],
        inverse[panel_index],
        precision=lax.Precision.HIGHEST,
        preferred_element_type=jnp.float32,
    )
    shared = from_root(lower_part.astype(jnp.bfloat16), COL, 0)
    return (lower_part, shared)


def apply_update(
    matrix, shared, upper_rows, finish, first_col, last_col, row_global, col_global, tile_mask
):
    if last_col <= first_col:
        return matrix
    row_count = matrix.shape[0]
    product = jnp.dot(shared, upper_rows[:, first_col:last_col], preferred_element_type=jnp.float32)
    width = last_col - first_col
    pattern_part = tile_mask[:, first_col // TILE : last_col // TILE]
    product = (
        product.reshape(row_count // TILE, TILE, width // TILE, TILE)
        * pattern_part[:, None, :, None]
    ).reshape(row_count, width)
    active_mask = (row_global >= finish)[:, None] & (col_global[first_col:last_col] >= finish)[
        None, :
    ]
    return matrix.at[:, first_col:last_col].add(-jnp.where(active_mask, product, 0.0))


def body(front_in, child_tiles, child_map, pattern, pivot_inverse):
    row_count, col_count = front_in.shape
    grid_rows = lax.axis_size("row")
    grid_cols = lax.axis_size(COL)
    groups = grid_rows * grid_cols
    row_index = lax.axis_index("row")
    col_index = lax.axis_index(COL)
    tile_rows = row_count // TILE
    tile_cols = col_count // TILE
    outgoing = child_tiles.reshape(grid_rows, grid_cols, SLOTS, TILE, TILE)
    targets = child_map.reshape(grid_rows, grid_cols, SLOTS)
    arrived, placed = (
        cut_exchange(outgoing.reshape(groups, SLOTS, TILE, TILE), ROW_COL, 2, 0, 0),
        cut_exchange(targets.reshape(groups, SLOTS), ROW_COL, 2, 0, 0),
    )
    child_flat = arrived.reshape(-1, TILE, TILE).astype(jnp.float32)
    flat_targets = placed.reshape(-1)
    local_row = flat_targets // NT - row_index * tile_rows
    local_col = flat_targets % NT - col_index * tile_cols
    matrix = (
        front_in.reshape(tile_rows, TILE, tile_cols, TILE)
        .at[local_row, :, local_col, :]
        .add(child_flat)
        .reshape(row_count, col_count)
    )
    row_global = row_index * row_count + jnp.arange(row_count)
    col_global = col_index * col_count + jnp.arange(col_count)
    tile_mask = lax.dynamic_slice(
        pattern, (row_index * tile_rows, col_index * tile_cols), (tile_rows, tile_cols)
    ).astype(jnp.float32)
    lower_part, shared = factor_panel(matrix, pivot_inverse, 0)
    for panel_index in range(PANELS):
        first_col = panel_index * PANEL
        finish = first_col + PANEL
        upper_rows = spread(matrix[first_col:finish, :].astype(jnp.bfloat16), "row", 0)
        stored = (row_global >= finish)[:, None] & (col_index == 0)
        matrix = matrix.at[:, first_col:finish].set(
            jnp.where(stored, lower_part, matrix[:, first_col:finish])
        )
        if panel_index + 1 < PANELS:
            matrix = apply_update(
                matrix,
                shared,
                upper_rows,
                finish,
                finish,
                finish + PANEL,
                row_global,
                col_global,
                tile_mask,
            )
            following = factor_panel(matrix, pivot_inverse, panel_index + 1)
            matrix = apply_update(
                matrix, shared, upper_rows, finish, 0, finish, row_global, col_global, tile_mask
            )
            matrix = apply_update(
                matrix,
                shared,
                upper_rows,
                finish,
                finish + PANEL,
                col_count,
                row_global,
                col_global,
                tile_mask,
            )
        else:
            matrix = apply_update(
                matrix, shared, upper_rows, finish, 0, col_count, row_global, col_global, tile_mask
            )
            following = (lower_part, shared)
        lower_part, shared = following
    return matrix


def solution(mesh):
    torus = Mesh(
        mesh.devices.reshape(mesh.shape["front"], mesh.shape["row"], 4, 2),
        ("front", "row", "col_0", "col_1"),
    )
    placed = (
        P(("front", "row"), COL),
        P(FRONT_ROW_COL, None, None, None),
        P(FRONT_ROW_COL, None),
        P("front", None),
        P("front", None, None),
    )
    return jax.shard_map(
        body, mesh=torus, in_specs=placed, out_specs=P(("front", "row"), COL), check_vma=False
    )
```

profile of v0, /device:TPU:47, one launch (start us, length us, event | category | flops | bytes accessed | tf_op | source)
XLA Modules:
  0.0 443.8 jit_solution(7594469492940474296)
XLA Ops:
  7.4 0.5 broadcast.330
  7.9 1.3 reduce.23
  9.2 0.7 reshape_reshape_reshape.6
  10.0 8.4 %all-to-all-start = ((s32[32,1,7]{2,1,0:T(1,128)}), s32[32,1,7]{2,1,0:T(1,128)S(1)}, u32[]{:S(2)}, u32[]{:S(2)}) async-start(s32[32,1,7]{2,1,0:T(1,128)} %bitcast), calls=%async_computation | async-start | bytes 32768 | tf_op jit(solution)/shard_map/all_to_all | solution.py:49
  18.4 8.1 %fusion.26 = (bf16[32,1,7,64,128]{4,3,2,1,0:T(8,128)(2,1)}, bf16[32,1,7,64,128]{4,3,2,1,0:T(8,128)(2,1)}) fusion(bf16[32,1,7,128,128]{4,3,2,1,0:T(8,128)(2,1)} %bitcast.72), kind=kLoop, calls=%fused_computation.61 | loop fusion | bytes 14680064 | tf_op jit(solution)/shard_map/split | solution.py:47
  26.5 50.9 %all_to_all.15 = bf16[32,1,7,64,128]{4,3,2,1,0:T(8,128)(2,1)} all-to-all(bf16[32,1,7,64,128]{4,3,2,1,0:T(8,128)(2,1)} %get-tuple-element.73), channel_id=1, replica_groups=mesh['front'=4,'row'=4,'col_0'=4,'col_1'=2] {'row','col_0','col_1'}, dimensions={0} | all-to-all | bytes 7340032 | tf_op jit(solution)/shard_map/all_to_all | solution.py:49
  77.4 6.2 %all-to-all-start.2 = ((bf16[32,1,7,64,128]{4,3,2,1,0:T(8,128)(2,1)}), bf16[32,1,7,64,128]{4,3,2,1,0:T(8,128)(2,1)}, u32[]{:S(2)}, u32[]{:S(2)}) async-start(bf16[32,1,7,64,128]{4,3,2,1,0:T(8,128)(2,1)} %get-tuple-element.74), calls=%async_computation.2 | async-start | bytes 7340032 | tf_op jit(solution)/shard_map/all_to_all | solution.py:49
  83.5 0.2 reduce-scatter.3.cloned.1.call-start
  83.8 5.5 %copy.14 = f32[256,8,8,128]{3,2,1,0:T(8,128)S(1)} copy(f32[256,8,8,128]{3,1,2,0:T(8,128)} %bitcast.71) | data formatting | bytes 16777216
  89.2 4.9 %copy.11 = f32[16,128,8,128]{3,1,2,0:T(8,128)} copy(f32[16,128,8,128]{3,2,1,0:T(8,128)S(1)} %bitcast.68) | data formatting | bytes 16777216 | tf_op jit(solution)/shard_map/reshape | solution.py:120
  94.1 0.7 reduce.24
  94.8 0.1 reshape_reshape.4
  94.9 33.4 %all-to-all-done.2 = bf16[32,1,7,64,128]{4,3,2,1,0:T(8,128)(2,1)} async-done(((bf16[32,1,7,64,128]{4,3,2,1,0:T(8,128)(2,1)}), bf16[32,1,7,64,128]{4,3,2,1,0:T(8,128)(2,1)}, u32[]{:S(2)}, u32[]{:S(2)}) %all-to-all-start.2) | async-done | bytes 3670048 | tf_op jit(solution)/shard_map/all_to_all | solution.py:49
  128.3 8.9 %pad_maximum_fusion = bf16[32,1,7,128,128]{4,3,2,1,0:T(8,128)(2,1)} fusion(bf16[32,1,7,64,128]{4,3,2,1,0:T(8,128)(2,1)} %all-to-all-done.2, bf16[32,1,7,64,128]{4,3,2,1,0:T(8,128)(2,1)} %all_to_all.15), kind=kLoop, calls=%fused_computation.6 | loop fusion | flops 14680064 | bytes 14680064 | tf_op jit(solution)/shard_map/concatenate | solution.py:50
  137.2 10.1 %bitcast_convert_fusion = f32[224,128,128]{2,1,0:T(8,128)} fusion(bf16[32,1,7,128,128]{4,3,2,1,0:T(8,128)(2,1)} %pad_maximum_fusion), kind=kLoop, calls=%fused_computation.7 | loop fusion | flops 3670016 | bytes 22020096 | tf_op jit(solution)/shard_map/convert_element_type | solution.py:115
  147.3 47.0 %scatter_fusion = f32[16,128,8,128]{3,1,2,0:T(8,128)} fusion(f32[16,128,8,128]{3,1,2,0:T(8,128)} %copy.11, s32[224]{0:T(256)S(1)} %bitcast.70, f32[224,128,128]{2,1,0:T(8,128)} %bitcast_convert_fusion), kind=kCustom, calls=%fused_computation | custom fusion | flops 3670016 | bytes 44041984 | tf_op jit(solution)/shard_map/scatter-add | solution.py:122
  194.2 1.7 fusion.13
  195.9 0.7 copy.13
  196.6 1.3 copy.26
  198.0 0.3 all-reduce.5.cloned.1.call-start
  198.3 9.9 %copy.12 = f32[16,128,8,128]{3,2,1,0:T(8,128)S(1)} copy(f32[16,128,8,128]{3,1,2,0:T(8,128)} %scatter_fusion) | data formatting | bytes 16777216 | tf_op jit(solution)/shard_map/scatter-add | solution.py:122
  208.2 2.1 copy.25
  210.3 8.9 %convert_select_fusion.1 = (bf16[2048,512]{1,0:T(8,128)(2,1)}, f32[2048,512]{1,0:T(8,128)}) fusion(pred[]{:T(512)S(6)} %eq.6, f32[2,512,512]{2,1,0:T(8,128)S(1)} %copy-done.2, f32[2048,1024]{1,0:T(8,128)S(1)} %bitcast.64), kind=kOutput, calls=%fused_computation.26 | convolution fusion | flops 6444548096 | bytes 11534337 | tf_op jit(solution)/shard_map/dot_general | solution.py:71
  219.3 0.6 reduce-scatter.3.cloned.1.call-done
  219.9 0.1 all-gather.3.cloned.1.call-update
  220.0 0.0 all-reduce.7.cloned.1.call-start
  220.1 58.2 %all-reduce.5.cloned.1.call-done = bf16[2048,512]{1,0:T(8,128)(2,1)} async-done(((bf16[2048,512]{1,0:T(8,128)(2,1)}), bf16[2048,512]{1,0:T(8,128)(2,1)}) %all-reduce.5.cloned.1.call-update) | async-done | bytes 2097168 | tf_op jit(solution)/shard_map/psum | solution.py:20
  278.3 0.7 compare_reduce_fusion
  279.1 0.8 dynamic-slice_convert_fusion
  279.9 0.1 fusion.27
  279.9 5.8 %fusion.3 = f32[2048,1024]{1,0:T(8,128)} fusion(f32[2048,1024]{1,0:T(8,128)} %bitcast.65, f32[2048,512]{1,0:T(8,128)} %get-tuple-element.80, pred[2048]{0:T(1024)(128)(4,1)S(1)} %get-tuple-element.86, pred[]{:T(512)} %compare_reduce_fusion), kind=kLoop, calls=%fused_computation.10 | loop fusion | flops 2097152 | bytes 12585472 | tf_op jit(solution)/shard_map/scatter | solution.py:136
  285.7 23.1 %all-reduce.7.cloned.1.call-done = bf16[2048,512]{1,0:T(8,128)(2,1)} async-done(((bf16[2048,512]{1,0:T(8,128)(2,1)}), bf16[2048,512]{1,0:T(8,128)(2,1)}) %all-reduce.7.cloned.1.call-update) | async-done | bytes 2097168 | tf_op jit(solution)/shard_map/psum | solution.py:20
  308.8 0.6 mul.57
  309.5 1.0 copy-done.3
  310.4 5.9 %constant_dynamic-update-slice_fusion = (f32[2048,1024]{1,0:T(8,128)}, f32[2048,512]{1,0:T(8,128)}) fusion(f32[2048,1024]{1,0:T(8,128)} %fusion.3, f32[256,8,4,128]{3,2,1,0:T(4,128)S(1)} %bitcast.69, bf16[2048,512]{1,0:T(8,128)(2,1)S(1)} %copy-done.3, bf16[512,1024]{1,0:T(8,128)(2,1)S(1)} %copy-done.4, pred[512]{0:T(512)(128)(4,1)S(1)} %get-tuple-element.78, ...), kind=kOutput, calls=%fused_computation.60 | convolution fusion | flops 1078984704 | bytes 19401216 | tf_op jit(solution)/shard_map/dot_general | solution.py:87
  316.3 0.6 mul.60
  316.9 5.5 %fusion.4 = f32[2048,1024]{1,0:T(8,128)} fusion(f32[2048,1024]{1,0:T(8,128)} %get-tuple-element.81, f32[256,8,4,128]{3,2,1,0:T(4,128)S(1)} %bitcast.73, bf16[2048,512]{1,0:T(8,128)(2,1)S(1)} %copy-done.3, pred[512]{0:T(512)(128)(4,1)S(1)} %get-tuple-element.77, pred[]{:T(512)} %compare_reduce_fusion, pred[2048]{0:T(1024)(128)(4,1)S(1)} %get-tuple-element.85, ...), kind=kOutput, calls=%fused_computation.11 | convolution fusion | flops 1080033280 | bytes 15207424 | tf_op jit(solution)/shard_map/dot_general | solution.py:87
  322.4 2.7 fusion.14
  325.1 0.0 all-reduce.9.cloned.1.call-start
  325.2 10.4 %fusion.10 = (f32[2048,1024]{1,0:T(8,128)}, bf16[2048,512]{1,0:T(8,128)(2,1)S(1)}) fusion(f32[2048,1024]{1,0:T(8,128)} %fusion.4, pred[2048]{0:T(1024)(128)(4,1)S(1)} %broadcast_and_fusion, f32[2048,512]{1,0:T(8,128)} %get-tuple-element.82, f32[2,512,512]{2,1,0:T(8,128)S(1)} %copy-done.2), kind=kOutput, calls=%fused_computation.20 | convolution fusion | flops 6444548096 | bytes 15730688 | tf_op jit(solution)/shard_map/dot_general | solution.py:71
  335.6 1.5 convert_select_fusion
  337.2 9.1 %reduce-scatter.5.cloned.1.call-done = bf16[128,1024]{1,0:T(8,128)(2,1)} async-done(((bf16[512,1024]{1,0:T(8,128)(2,1)}), bf16[128,1024]{1,0:T(8,128)(2,1)}) %reduce-scatter.5.cloned.1.call-update) | async-done | bytes 262160 | tf_op jit(solution)/shard_map/reduce_scatter | solution.py:65
  346.3 0.0 all-reduce.11.cloned.1.call-start
  346.4 49.0 %all-reduce.9.cloned.1.call-done = bf16[2048,512]{1,0:T(8,128)(2,1)} async-done(((bf16[2048,512]{1,0:T(8,128)(2,1)}), bf16[2048,512]{1,0:T(8,128)(2,1)}) %all-reduce.9.cloned.1.call-update) | async-done | bytes 2097168 | tf_op jit(solution)/shard_map/psum | solution.py:20
  395.4 30.5 %all-reduce.11.cloned.1.call-done = bf16[2048,512]{1,0:T(8,128)(2,1)} async-done(((bf16[2048,512]{1,0:T(8,128)(2,1)}), bf16[2048,512]{1,0:T(8,128)(2,1)}) %all-reduce.11.cloned.1.call-update) | async-done | bytes 2097168 | tf_op jit(solution)/shard_map/psum | solution.py:20
  425.9 0.6 mul.63
  426.5 2.8 copy-done.1
  429.3 7.2 %fusion.2 = f32[2048,1024]{1,0:T(8,128)} fusion(f32[2048,1024]{1,0:T(8,128)S(1)} %copy-done.1, f32[256,8,8,128]{3,2,1,0:T(8,128)S(1)} %bitcast.66, bf16[2048,512]{1,0:T(8,128)(2,1)} %all-reduce.11.cloned.1.call-done, bf16[512,1024]{1,0:T(8,128)(2,1)} %all-gather.5.cloned.1.call-done, pred[1024]{0:T(1024)(128)(4,1)S(1)} %broadcast_compare_fusion, ...), kind=kOutput, calls=%fused_computation.4 | convolution fusion | flops 2157969408 | bytes 28314624 | tf_op jit(solution)/shard_map/dot_general | solution.py:87
  (28 shorter events, 0.4 us)
Async XLA Ops:
  10.0 16.5 %all-to-all-start = ((s32[32,1,7]{2,1,0:T(1,128)}), s32[32,1,7]{2,1,0:T(1,128)S(1)}, u32[]{:S(2)}, u32[]{:S(2)}) async-start(s32[32,1,7]{2,1,0:T(1,128)} %bitcast), calls=%async_computation | async-start | bytes 32768 | tf_op jit(solution)/shard_map/all_to_all | solution.py:49
  77.4 50.9 %all-to-all-start.2 = ((bf16[32,1,7,64,128]{4,3,2,1,0:T(8,128)(2,1)}), bf16[32,1,7,64,128]{4,3,2,1,0:T(8,128)(2,1)}, u32[]{:S(2)}, u32[]{:S(2)}) async-start(bf16[32,1,7,64,128]{4,3,2,1,0:T(8,128)(2,1)} %get-tuple-element.74), calls=%async_computation.2 | async-start | bytes 7340032 | tf_op jit(solution)/shard_map/all_to_all | solution.py:49
  83.5 136.4 %reduce-scatter.3.cloned.1.call-start = ((), (), s32[]{:S(2)}) async-start(), calls=%async_computation.7 | async-start | bytes 1310720 | tf_op jit(solution)/shard_map/reduce_scatter | solution.py:65
  198.0 80.3 %all-reduce.5.cloned.1.call-start = ((), (), s32[]{:S(2)}) async-start(), calls=%async_computation.5 | async-start | bytes 4194304 | tf_op jit(solution)/shard_map/psum | solution.py:20
  208.2 2.2 copy-start.2
  210.3 8.9 %copy-start = (f32[256,8,8,128]{3,1,2,0:T(8,128)}, f32[256,8,8,128]{3,1,2,0:T(8,128)S(1)}, u32[]{:S(2)}) copy-start(f32[256,8,8,128]{3,1,2,0:T(8,128)S(1)} %copy.25) | copy-start | bytes 25165828
  219.3 66.4 %all-gather.3.cloned.1.call-start = ((), (), s32[]{:S(2)}) async-start(), calls=%async_computation.8 | async-start | bytes 1310720 | tf_op jit(solution)/shard_map/all_gather | solution.py:66
  220.0 88.8 %all-reduce.7.cloned.1.call-start = ((), (), s32[]{:S(2)}) async-start(), calls=%async_computation.6 | async-start | bytes 4194304 | tf_op jit(solution)/shard_map/psum | solution.py:20
  278.3 68.0 %reduce-scatter.5.cloned.1.call-start = ((), (), s32[]{:S(2)}) async-start(), calls=%async_computation.11 | async-start | bytes 1310720 | tf_op jit(solution)/shard_map/reduce_scatter | solution.py:65
  285.7 23.7 %copy-start.4 = (bf16[512,1024]{1,0:T(8,128)(2,1)S(1)}, bf16[512,1024]{1,0:T(8,128)(2,1)}, u32[]{:S(2)}) copy-start(bf16[512,1024]{1,0:T(8,128)(2,1)} %all-gather.3.cloned.1.call-done) | copy-start | bytes 3145732
  308.8 1.6 copy-start.3
  325.1 70.2 %all-reduce.9.cloned.1.call-start = ((), (), s32[]{:S(2)}) async-start(), calls=%async_computation.9 | async-start | bytes 4194304 | tf_op jit(solution)/shard_map/psum | solution.py:20
  337.1 58.3 %all-gather.5.cloned.1.call-start = ((), (), s32[]{:S(2)}) async-start(), calls=%async_computation.12 | async-start | bytes 1310720 | tf_op jit(solution)/shard_map/all_gather | solution.py:66
  346.3 79.6 %all-reduce.11.cloned.1.call-start = ((), (), s32[]{:S(2)}) async-start(), calls=%async_computation.10 | async-start | bytes 4194304 | tf_op jit(solution)/shard_map/psum | solution.py:20
  425.9 3.4 copy-start.1
Sparse Core Ops, SparseCore 0:
  198.1 21.7 reduce-scatter.2
  221.9 24.6 all-gather.2
  325.2 21.0 reduce-scatter.4
  347.8 24.9 all-gather.4
Sparse Core Ops, SparseCore 1:
  219.4 58.8 all-reduce.4
  280.7 28.0 all-reduce.6
  337.2 58.1 all-reduce.8
  397.8 28.0 all-reduce.10
where the time goes:
time: 446 us; the launch traced here: 444 us
  waiting for transfers between devices  204 us (46%)
  other arithmetic  81.1 us (18%)
  blocking collectives  50.9 us (11%)
  local copies, waits for them, and re-layouts  39.5 us (9%)
  matrix products  37.9 us (8%)
  starting transfers between devices  15.3 us (3%)
  between operations  15 us (3%)
    psum x4, waiting for transfers between devices, from_root(): x = lax.psum(x, axis)  161 us
    all_to_all x1, blocking collectives, cut_exchange(): lax.all_to_all(piece, axis, split_axis=0, concat_axis=0, tiled=True)  50.9 us
    scatter-add x1, other arithmetic, body(): matrix = front_in.reshape(tile_rows, TILE, tile_cols, TILE).at[local_row,...  47 us
    all_to_all x2, waiting for transfers between devices, cut_exchange(): lax.all_to_all(piece, axis, split_axis=0, concat_axis=0, tiled=True)  33.4 us
    dot_general x2, matrix products, factor_panel(): jnp.dot(matrix[:, first_col:first_col + PANEL], inverse[panel_index], pre...  19.4 us
    dot_general x3, matrix products, apply_update(): jnp.dot(shared, upper_rows[:, first_col:last_col], preferred_element_type...  18.5 us
    all_to_all x2, starting transfers between devices, cut_exchange(): lax.all_to_all(piece, axis, split_axis=0, concat_axis=0, tiled=True)  14.6 us
    unnamed x14, local copies, waits for them, and re-layouts  13.2 us
  transfers between devices with their start and end apart: 10, of which 7 were waited for; matrix products, arithmetic and copies ran while one was open for 13% of the time, Pallas kernels for 0%

commit v1 on v0

v1 whole, which is shorter than its diff:
```python
import functools

import jax
import jax.numpy as jnp
from jax import lax
from jax.experimental import pallas as pl
from jax.experimental.pallas import tpu as pltpu
from jax.sharding import PartitionSpec as P

TILE = 128
PANEL = 512
SLOTS = 7
NT = 64
ROWS = 2048
COLS = 1024
MESH = pl.DeviceIdType.MESH
ANY = pl.BlockSpec(memory_space=pl.ANY)
VMEM = pl.BlockSpec(memory_space=pltpu.VMEM)
SMEM = pl.BlockSpec(memory_space=pltpu.SMEM)
F32 = jnp.float32
BF16 = jnp.bfloat16


def position():
    col = lax.axis_index("col")
    return lax.axis_index("front"), lax.axis_index("row"), col // 2, lax.rem(col, 2)


def mod4(v):
    return lax.rem(v + 8, 4)


def device(x, y, z, k):
    return (x, mod4(y), mod4(z) * 2 + k)


def remote(src, dst, send, recv, to):
    return pltpu.make_async_remote_copy(src, dst, send, recv, device_id=to, device_id_type=MESH)


def greet(peers):
    barrier = pltpu.get_barrier_semaphore()
    for peer in peers:
        pl.semaphore_signal(barrier, inc=1, device_id=peer, device_id_type=MESH)
    pl.semaphore_wait(barrier, len(peers))


STEPS = (1, 3, 2)


def exchange_kernel(src, dst, mid, send, recv, local):
    x, y, z, k = position()
    other = 1 - k
    greet(
        [device(x, y + d, z, c) for d in STEPS for c in (k, other)]
        + [device(x, y, z + d, c) for d in STEPS for c in (k, other)]
        + [device(x, y, z, other)]
    )
    count = 0

    def send_to(block, target, to):
        nonlocal count
        copy = remote(block, target, send.at[count], recv.at[count], to)
        copy.start()
        count += 1
        return copy

    first = []
    for a in STEPS:
        for b in STEPS:
            first.append(
                (
                    send_to(src.at[mod4(y + a), mod4(z + b), k], mid.at[0, a, b], device(x, y + a, z, k)),
                    send_to(
                        src.at[mod4(y + b), mod4(z + a), other], mid.at[1, a, b], device(x, y, z + a, other)
                    ),
                    a,
                    b,
                )
            )
    rest = []
    for d in STEPS:
        rest.append(send_to(src.at[mod4(y + d), z, k], dst.at[y, z, k], device(x, y + d, z, k)))
        rest.append(send_to(src.at[y, mod4(z + d), k], dst.at[y, z, k], device(x, y, z + d, k)))
        rest.append(send_to(src.at[mod4(y + d), z, other], dst.at[y, z, k], device(x, y + d, z, other)))
        rest.append(send_to(src.at[y, mod4(z + d), other], dst.at[y, z, k], device(x, y, z + d, other)))
    rest.append(send_to(src.at[y, z, other], dst.at[y, z, k], device(x, y, z, other)))
    own = pltpu.make_async_copy(src.at[y, z, k], dst.at[y, z, k], local)
    own.start()
    for by_row, by_col, a, b in first:
        by_row.wait_recv()
        rest.append(send_to(mid.at[0, a, b], dst.at[mod4(y - a), z, k], device(x, y, z + b, k)))
        by_col.wait_recv()
        rest.append(send_to(mid.at[1, a, b], dst.at[y, mod4(z - a), other], device(x, y + b, z, k)))
    for by_row, by_col, _, _ in first:
        by_row.wait_send()
        by_col.wait_send()
    own.wait()
    for copy in rest:
        copy.wait()


def exchange(tiles):
    shape = (4, 4, 2, SLOTS, TILE, TILE)
    copies = 18 + 13 + 18
    return pl.pallas_call(
        exchange_kernel,
        out_shape=(
            jax.ShapeDtypeStruct(shape, tiles.dtype),
            jax.ShapeDtypeStruct((2, 4, 4, SLOTS, TILE, TILE), tiles.dtype),
        ),
        in_specs=[ANY],
        out_specs=(ANY, ANY),
        scratch_shapes=[
            pltpu.SemaphoreType.DMA((copies,)),
            pltpu.SemaphoreType.DMA((copies,)),
            pltpu.SemaphoreType.DMA,
        ],
        compiler_params=pltpu.CompilerParams(collective_id=0, has_side_effects=True),
        name="exchange",
    )(tiles.reshape(shape))[0]


def split(x):
    high = x.astype(BF16)
    return high, (x - high.astype(F32)).astype(BF16)


def wide_dot(a, b):
    a_high, a_low = split(a)
    b_high, b_low = split(b)
    dot = functools.partial(jnp.dot, preferred_element_type=F32)
    return dot(a_high, b_high) + (dot(a_low, b_high) + dot(a_high, b_low))


KIDS = 28


def assemble_kernel(target, front, kids, inverse, full, lower, upper, acc, kid_buf, inv, low, up, sems):
    row = lax.axis_index("row")
    col = lax.axis_index("col")
    groups = 224 // KIDS
    loads = [
        pltpu.make_async_copy(
            front.at[pl.ds(256 * i, 256)], acc.at[pl.ds(256 * i, 256)], sems.at[i]
        )
        for i in range(8)
    ]
    kid_loads = [
        pltpu.make_async_copy(kids.at[pl.ds(KIDS * i, KIDS)], kid_buf.at[pl.ds(KIDS * i, KIDS)], sems.at[8 + i])
        for i in range(groups)
    ]
    for copy in loads + kid_loads:
        copy.start()
    inv_load = pltpu.make_async_copy(inverse.at[0], inv, sems.at[16])
    inv_load.start()
    for copy in loads:
        copy.wait()
    for g in range(groups):
        kid_loads[g].wait()

        def add(i, _):
            t = target[i]
            r = pl.multiple_of((t // 8) * TILE, TILE)
            c = pl.multiple_of(lax.rem(t, 8) * TILE, TILE)
            acc[pl.ds(r, TILE), pl.ds(c, TILE)] += kid_buf[i].astype(F32)
            return 0

        lax.fori_loop(KIDS * g, KIDS * (g + 1), add, 0, unroll=2)
    inv_load.wait()
    right = pltpu.make_async_copy(acc.at[:, pl.ds(PANEL, PANEL)], full.at[:, pl.ds(PANEL, PANEL)], sems.at[0])
    right.start()

    up[...] = acc[0:PANEL, :].astype(BF16)
    up_out = pltpu.make_async_copy(up, upper, sems.at[3])
    up_out.start()

    @pl.when(col == 0)
    def _():
        @pl.loop(0, ROWS // 256)
        def _(i):
            rows = pl.ds(pl.multiple_of(i * 256, 256), 256)
            part = wide_dot(acc[rows, 0:PANEL], inv[...])
            low[rows, :] = part.astype(BF16)

            @pl.when((row > 0) | (i >= 2))
            def _():
                acc[rows, 0:PANEL] = part

    left = pltpu.make_async_copy(acc.at[:, pl.ds(0, PANEL)], full.at[:, pl.ds(0, PANEL)], sems.at[1])
    left.start()
    low_out = pltpu.make_async_copy(low, lower, sems.at[2])
    low_out.start()
    for copy in (right, left, low_out, up_out):
        copy.wait()


def assemble(target, front, kids, inverse):
    return pl.pallas_call(
        assemble_kernel,
        out_shape=(
            jax.ShapeDtypeStruct((ROWS, COLS), F32),
            jax.ShapeDtypeStruct((ROWS, PANEL), BF16),
            jax.ShapeDtypeStruct((PANEL, COLS), BF16),
        ),
        in_specs=[SMEM, ANY, ANY, ANY],
        out_specs=(ANY, ANY, ANY),
        scratch_shapes=[
            pltpu.VMEM((ROWS, COLS), F32),
            pltpu.VMEM((224, TILE, TILE), BF16),
            pltpu.VMEM((PANEL, PANEL), F32),
            pltpu.VMEM((ROWS, PANEL), BF16),
            pltpu.VMEM((PANEL, COLS), BF16),
            pltpu.SemaphoreType.DMA((17,)),
        ],
        compiler_params=pltpu.CompilerParams(vmem_limit_bytes=40 << 20),
        name="assemble",
    )(target, front, kids, inverse)


PIECES = 8


def lower_piece(ref, panel, way, i):
    chunk = lax.rem(i // 2 + 1, 4) * 4 + 2 * way + lax.rem(i, 2)
    return ref.at[pl.ds(pl.multiple_of(chunk * 128, 128), 128), pl.ds(panel * PANEL, PANEL)]


def upper_piece(ref, panel, way, i):
    chunk = lax.rem(i // 4 * 4 + 4, 8) + 2 * way + lax.rem(i, 4) // 2
    start = panel * PANEL + lax.rem(i, 2) * 256
    return ref.at[
        pl.ds(pl.multiple_of(start, 256), 256), pl.ds(pl.multiple_of(chunk * TILE, TILE), TILE)
    ]


def share_kernel(
    full, low_in, up_in, inverse, mask, full_out, low, up,
    panel_cols, panel_rows, inv, part, send_low, recv_low, send_core, send_up, recv_up, sems
):
    x, y, z, k = position()
    other = 1 - k
    first_row = y == 0
    first_col = (z == 0) & (k == 0)
    right = device(x, y, z + 1, k), device(x, y, z - 1, k)
    down = device(x, y + 1, z, k), device(x, y - 1, z, k)
    across = device(x, y, z, other)
    low_hops = z, mod4(-z)
    up_hops = y, mod4(-y)
    loads = [
        pltpu.make_async_copy(full.at[:, pl.ds(PANEL, PANEL)], panel_cols, sems.at[0]),
        pltpu.make_async_copy(full.at[pl.ds(PANEL, PANEL), :], panel_rows, sems.at[1]),
        pltpu.make_async_copy(inverse.at[1], inv, sems.at[2]),
    ]

    for copy in loads:
        copy.start()

    @pl.when(first_col)
    def _():
        copy = pltpu.make_async_copy(low_in, low.at[:, pl.ds(0, PANEL)], sems.at[3])
        copy.start()
        copy.wait()

    @pl.when(first_row)
    def _():
        copy = pltpu.make_async_copy(up_in, up.at[pl.ds(0, PANEL)], sems.at[4])
        copy.start()
        copy.wait()

    greet([*right, *down, across])

    def low_copy(panel, way, i):
        n = (panel * 2 + way) * PIECES + i
        piece = lower_piece(low, panel, way, i)
        return remote(piece, piece, send_low.at[n], recv_low.at[n], right[way])

    def core_copy(panel, way, i):
        n = (panel * 2 + way) * PIECES + i
        piece = lower_piece(low, panel, way, i)
        return remote(piece, piece, send_core.at[n], recv_low.at[n], across)

    def up_copy(panel, way, i):
        n = (panel * 2 + way) * PIECES + i
        piece = upper_piece(up, panel, way, i)
        return remote(piece, piece, send_up.at[n], recv_up.at[n], down[way])

    def phase(panel):
        @pl.loop(0, PIECES + 4)
        def _(t):
            for way in (0, 1):
                i = t - up_hops[way]

                @pl.when((i >= 0) & (i < PIECES))
                def _():
                    @pl.when(y != 0)
                    def _():
                        up_copy(panel, way, i).wait_recv()

                    @pl.when(up_hops[way] < 3)
                    def _():
                        up_copy(panel, way, i).start()

                j = t - low_hops[way] - k

                @pl.when((j >= 0) & (j < PIECES))
                def _():
                    @pl.when(jnp.logical_not(first_col))
                    def _():
                        low_copy(panel, way, j).wait_recv()

                    @pl.when((k == 0) & (low_hops[way] < 3))
                    def _():
                        low_copy(panel, way, j).start()

                    @pl.when(k == 0)
                    def _():
                        core_copy(panel, way, j).start()

    phase(0)
    for copy in loads:
        copy.wait()

    @pl.when(first_row)
    def _():
        for n in range(PANEL // TILE):
            rows = slice(n * TILE, (n + 1) * TILE)
            cut = jnp.dot(
                low[PANEL + n * TILE : PANEL + (n + 1) * TILE, 0:PANEL], up[0:PANEL, :], preferred_element_type=F32
            )
            value = panel_rows[rows, :] - cut * mask[4 + n : 5 + n, :]

            @pl.when(first_col)
            def _():
                panel_rows[rows, PANEL:] = value[:, PANEL:]

            @pl.when(jnp.logical_not(first_col))
            def _():
                panel_rows[rows, :] = value

            up[PANEL + n * TILE : PANEL + (n + 1) * TILE, :] = value.astype(BF16)

    @pl.when(first_col)
    def _():
        for n in range(ROWS // TILE):
            rows = slice(n * TILE, (n + 1) * TILE)
            cut = jnp.dot(low[rows, 0:PANEL], up[0:PANEL, PANEL:], preferred_element_type=F32)
            value = panel_cols[rows, :] - cut * mask[n : n + 1, PANEL:]
            part[rows, :] = wide_dot(value, inv[...])
            low[rows, PANEL:] = part[rows, :].astype(BF16)
    phase(1)

    @pl.when(first_col)
    def _():
        @pl.when(first_row)
        def _():
            copy = pltpu.make_async_copy(
                part.at[pl.ds(2 * PANEL, ROWS - 2 * PANEL)],
                full_out.at[pl.ds(2 * PANEL, ROWS - 2 * PANEL), pl.ds(PANEL, PANEL)],
                sems.at[0],
            )
            copy.start()
            copy.wait()

        @pl.when(jnp.logical_not(first_row))
        def _():
            copy = pltpu.make_async_copy(part, full_out.at[:, pl.ds(PANEL, PANEL)], sems.at[0])
            copy.start()
            copy.wait()

    @pl.when(first_row)
    def _():
        copy = pltpu.make_async_copy(panel_rows, full_out.at[pl.ds(PANEL, PANEL)], sems.at[1])
        copy.start()
        copy.wait()

    @pl.loop(0, PIECES)
    def _(i):
        for panel in (0, 1):
            for way in (0, 1):
                @pl.when(up_hops[way] < 3)
                def _():
                    up_copy(panel, way, i).wait_send()

                @pl.when((k == 0) & (low_hops[way] < 3))
                def _():
                    low_copy(panel, way, i).wait_send()

                @pl.when(k == 0)
                def _():
                    core_copy(panel, way, i).wait_send()


def share(full, low, up, inverse, mask):
    pieces = 2 * 2 * PIECES
    dma = pltpu.SemaphoreType.DMA((pieces,))
    return pl.pallas_call(
        share_kernel,
        out_shape=(
            jax.ShapeDtypeStruct((ROWS, COLS), F32),
            jax.ShapeDtypeStruct((ROWS, 2 * PANEL), BF16),
            jax.ShapeDtypeStruct((2 * PANEL, COLS), BF16),
        ),
        in_specs=[ANY, ANY, ANY, ANY, VMEM],
        out_specs=(ANY, VMEM, VMEM),
        scratch_shapes=[
            pltpu.VMEM((ROWS, PANEL), F32),
            pltpu.VMEM((PANEL, COLS), F32),
            pltpu.VMEM((PANEL, PANEL), F32),
            pltpu.VMEM((ROWS, PANEL), F32),
            dma,
            dma,
            dma,
            dma,
            dma,
            pltpu.SemaphoreType.DMA((5,)),
        ],
        input_output_aliases={0: 0},
        compiler_params=pltpu.CompilerParams(
            collective_id=1, has_side_effects=True, vmem_limit_bytes=48 << 20
        ),
        name="share",
    )(full, low, up, inverse, mask)


BLOCK = 256


def update_kernel(full, low, up, mask, out):
    skip = (lax.axis_index("col") == 0) | (
        (lax.axis_index("row") == 0) & (pl.program_id(0) < 2 * PANEL // BLOCK)
    )

    @pl.when(skip)
    def _():
        out[...] = full[...]

    @pl.when(jnp.logical_not(skip))
    def _():
        for n in range(BLOCK // TILE):
            rows = slice(n * TILE, (n + 1) * TILE)
            cut = jnp.dot(low[rows, :], up[...], preferred_element_type=F32)
            tile_row = pl.program_id(0) * (BLOCK // TILE) + n
            out[rows, :] = full[rows, :] - cut * mask[pl.ds(tile_row, 1), :]


def update(full, low, up, mask):
    return pl.pallas_call(
        update_kernel,
        out_shape=jax.ShapeDtypeStruct((ROWS, COLS), F32),
        grid=(ROWS // BLOCK,),
        in_specs=[
            pl.BlockSpec((BLOCK, COLS), lambda i: (i, 0)),
            pl.BlockSpec((BLOCK, 2 * PANEL), lambda i: (i, 0)),
            pl.BlockSpec((2 * PANEL, COLS), lambda i: (0, 0), pipeline_mode=pl.Buffered(1)),
            pl.BlockSpec((ROWS // TILE, COLS), lambda i: (0, 0), pipeline_mode=pl.Buffered(1)),
        ],
        out_specs=pl.BlockSpec((BLOCK, COLS), lambda i: (i, 0)),
        compiler_params=pltpu.CompilerParams(
            dimension_semantics=("arbitrary",), vmem_limit_bytes=32 << 20
        ),
        name="update",
    )(full, low, up, mask)


def body(front_in, child_tiles, child_map, pattern, pivot_inverse):
    row = lax.axis_index("row")
    col = lax.axis_index("col")
    tile_rows, tile_cols = ROWS // TILE, COLS // TILE
    placed = lax.all_to_all(
        child_map.reshape(32, SLOTS), ("row", "col"), split_axis=0, concat_axis=0, tiled=True
    ).reshape(-1)
    target = (placed // NT - row * tile_rows) * tile_cols + placed % NT - col * tile_cols
    mask = lax.dynamic_slice(
        pattern, (row * tile_rows, col * tile_cols), (tile_rows, tile_cols)
    ).astype(F32)
    mask = jnp.repeat(mask, TILE, axis=1)
    kids = exchange(child_tiles).reshape(-1, TILE, TILE)
    full, low, up = assemble(target, front_in, kids, pivot_inverse)
    full, low, up = share(full, low, up, pivot_inverse, mask)
    return update(full, low, up, mask)


def solution(mesh):
    return jax.shard_map(
        body,
        mesh=mesh,
        in_specs=(
            P(("front", "row"), "col"),
            P(("front", "row", "col"), None, None, None),
            P(("front", "row", "col"), None),
            P("front", None),
            P("front", None, None),
        ),
        out_specs=P(("front", "row"), "col"),
        check_vma=False,
    )
```

time: 446 us -> 210 us (0.47)
  waiting for transfers between devices: 204 us -> 0.01 us
  Pallas kernels: 0 us -> 188 us
  other arithmetic: 81.1 us -> 2.95 us
  blocking collectives: 50.9 us -> 0 us
  matrix products: 37.9 us -> 0 us
  local copies, waits for them, and re-layouts: 39.5 us -> 10.1 us
  between operations: 15 us -> 0.1 us
  starting transfers between devices: 15.3 us -> 8.41 us
    pallas_call x0 -> x4, Pallas kernels: none -> 188 us  [the longest x1 84.9 us: exchange(): pl.pallas_call(exchange_kernel, out_shape=(jax.ShapeDtypeStruct(shape, ti...]
    psum x4 -> x0, waiting for transfers between devices: 161 us -> none  [from_root(): x = lax.psum(x, axis)]
    all_to_all x1 -> x0, blocking collectives: 50.9 us -> none  [cut_exchange(): lax.all_to_all(piece, axis, split_axis=0, concat_axis=0, tiled=True)]
    scatter-add x1 -> x0, other arithmetic: 47 us -> none  [body(): matrix = front_in.reshape(tile_rows, TILE, tile_cols, TILE).at[local_row,...]
    dot_general x5 -> x0, matrix products: 37.9 us -> none  [the longest x2 19.4 us: factor_panel(): jnp.dot(matrix[:, first_col:first_col + PANEL], inverse[panel_index], pre...]
    all_to_all x2 -> x1, waiting for transfers between devices: 33.4 us -> 0.01 us  [body(): lax.all_to_all(child_map.reshape(32, SLOTS), ('row', 'col'), split_axis=0...]
    convert_element_type x2 -> x1, other arithmetic: 10.9 us -> 0.78 us  [body(): mask = lax.dynamic_slice(pattern, (row * tile_rows, col * tile_cols), (ti...]
    scatter-add x1 -> x0, local copies, waits for them, and re-layouts: 9.92 us -> none  [body(): matrix = front_in.reshape(tile_rows, TILE, tile_cols, TILE).at[local_row,...]
  transfers between devices with their start and end apart: 10 -> 1, of which waited for: 7 -> 0; matrix products, arithmetic and copies ran while one was open for 13% -> 0% of each run, Pallas kernels for 0% -> 40%
where the time goes in v1:
time: 210 us
  Pallas kernels  188 us (90%)
  local copies, waits for them, and re-layouts  10.1 us (5%)
  starting transfers between devices  8.41 us (4%)
  other arithmetic  2.95 us (1%)
    pallas_call x1, Pallas kernels, exchange(): pl.pallas_call(exchange_kernel, out_shape=(jax.ShapeDtypeStruct(shape, ti...  84.9 us
    pallas_call x1, Pallas kernels, share(): pl.pallas_call(share_kernel, out_shape=(jax.ShapeDtypeStruct((ROWS, COLS)...  84.7 us
    pallas_call x1, Pallas kernels, assemble(): pl.pallas_call(assemble_kernel, out_shape=(jax.ShapeDtypeStruct((ROWS, CO...  10.9 us
    unnamed x10, local copies, waits for them, and re-layouts  9.25 us
    all_to_all x1, starting transfers between devices, body(): lax.all_to_all(child_map.reshape(32, SLOTS), ('row', 'col'), split_axis=0...  8.41 us
    pallas_call x1, Pallas kernels, update(): pl.pallas_call(update_kernel, out_shape=jax.ShapeDtypeStruct((ROWS, COLS)...  7.62 us
  transfers between devices with their start and end apart: 1, of which 0 were waited for; matrix products, arithmetic and copies ran while one was open for 0% of the time, Pallas kernels for 40%

profile of v1, /device:TPU:47, one launch (start us, length us, event | category | flops | bytes accessed | tf_op | source)
XLA Modules:
  0.0 209.8 jit_solution(179576022345225999)
XLA Ops:
  0.0 0.0 copy-start.1
  0.0 0.6 broadcast.19
  0.6 1.4 reduce.6
  2.0 0.7 all_to_all.6
  2.7 8.4 %all-to-all-start = ((s32[32,1,7]{2,1,0:T(1,128)}), s32[32,1,7]{2,1,0:T(1,128)S(1)}, u32[]{:S(2)}, u32[]{:S(2)}) async-start(s32[32,1,7]{2,1,0:T(1,128)} %bitcast), calls=%async_computation | async-start | bytes 32768 | tf_op jit(solution)/shard_map/all_to_all | solution.py:470
  11.2 0.8 dynamic-slice_convert_fusion
  11.9 0.1 broadcast_in_dim.3
  12.0 84.9 %exchange.1 = (bf16[4,4,2,7,128,128]{5,4,3,2,1,0:T(8,128)(2,1)}, bf16[2,4,4,7,128,128]{5,4,3,2,1,0:T(8,128)(2,1)}) custom-call(bf16[4,4,2,7,128,128]{5,4,3,2,1,0:T(8,128)(2,1)} %bitcast.10), custom_call_target="tpu_custom_call" | custom-call | tf_op jit(solution)/shard_map/exchange/pallas_call | solution.py:106
  97.0 0.0 all-to-all-done
  97.0 0.7 reduce.7
  97.7 0.1 reshape.17
  97.8 0.0 copy-done.1
  97.9 0.0 copy-start.2
  97.9 3.1 %copy-done.2 = bf16[4,4,2,7,128,128]{5,4,3,2,1,0:T(8,128)(2,1)S(1)} copy-done((bf16[4,4,2,7,128,128]{5,4,3,2,1,0:T(8,128)(2,1)S(1)}, bf16[4,4,2,7,128,128]{5,4,3,2,1,0:T(8,128)(2,1)}, u32[]{:S(2)}) %copy-start.2) | copy-done | bytes 7340056
  100.9 10.9 %assemble.1 = (f32[2048,1024]{1,0:T(8,128)}, bf16[2048,512]{1,0:T(8,128)(2,1)S(1)}, bf16[512,1024]{1,0:T(8,128)(2,1)S(1)}) custom-call(s32[224]{0:T(256)S(1)} %fusion.1.target, f32[2048,1024]{1,0:T(8,128)} %front.1, bf16[224,128,128]{2,1,0:T(8,128)(2,1)S(1)} %bitcast.7, f32[2,512,512]{2,1,0:T(8,128)S(1)} %copy-done.1), custom_call_target="tpu_custom_call" | custom-call | tf_op jit(solution)/shard_map/assemble/pallas_call | solution.py:199
  111.9 84.7 %share.1 = (f32[2048,1024]{1,0:T(8,128)}, bf16[2048,1024]{1,0:T(8,128)(2,1)}, bf16[1024,1024]{1,0:T(8,128)(2,1)S(1)}) custom-call(f32[2048,1024]{1,0:T(8,128)} %get-tuple-element.13.full, bf16[2048,512]{1,0:T(8,128)(2,1)S(1)} %get-tuple-element.14.low_in, bf16[512,1024]{1,0:T(8,128)(2,1)S(1)} %get-tuple-element.15.up_in, ...), custom_call_target="tpu_custom_call", output_to_operand_aliasing={{0}: (0, {})} | custom-call | tf_op jit(solution)/shard_map/share/pallas_call | solution.py:397
  196.6 0.0 copy-start
  196.6 3.4 %copy-done = f32[2048,1024]{1,0:T(8,128)S(1)} copy-done((f32[2048,1024]{1,0:T(8,128)S(1)}, f32[2048,1024]{1,0:T(8,128)}, u32[]{:S(2)}) %copy-start) | copy-done | bytes 8388632
  200.0 0.0 copy-start.3
  200.0 2.2 %copy-done.3 = bf16[2048,1024]{1,0:T(8,128)(2,1)S(1)} copy-done((bf16[2048,1024]{1,0:T(8,128)(2,1)S(1)}, bf16[2048,1024]{1,0:T(8,128)(2,1)}, u32[]{:S(2)}) %copy-start.3) | copy-done | bytes 4194328
  202.2 7.6 %update.1 = f32[2048,1024]{1,0:T(8,128)} custom-call(f32[2048,1024]{1,0:T(8,128)S(1)} %copy-done, bf16[2048,1024]{1,0:T(8,128)(2,1)S(1)} %copy-done.3, bf16[1024,1024]{1,0:T(8,128)(2,1)S(1)} %get-tuple-element.18.up, f32[16,1024]{1,0:T(8,128)S(1)} %bitcast.9), custom_call_target="tpu_custom_call" | custom-call | tf_op jit(solution)/shard_map/update/pallas_call | solution.py:448
  (2 shorter events, 0.0 us)
Async XLA Ops:
  0.0 97.8 %copy-start.1 = (f32[2,512,512]{2,1,0:T(8,128)S(1)}, f32[2,512,512]{2,1,0:T(8,128)}, u32[]{:S(2)}) copy-start(f32[2,512,512]{2,1,0:T(8,128)} %inverse.3) | copy-start | bytes 6291460
  2.7 94.2 %all-to-all-start = ((s32[32,1,7]{2,1,0:T(1,128)}), s32[32,1,7]{2,1,0:T(1,128)S(1)}, u32[]{:S(2)}, u32[]{:S(2)}) async-start(s32[32,1,7]{2,1,0:T(1,128)} %bitcast), calls=%async_computation | async-start | bytes 32768 | tf_op jit(solution)/shard_map/all_to_all | solution.py:470
  97.9 3.1 %copy-start.2 = (bf16[4,4,2,7,128,128]{5,4,3,2,1,0:T(8,128)(2,1)S(1)}, bf16[4,4,2,7,128,128]{5,4,3,2,1,0:T(8,128)(2,1)}, u32[]{:S(2)}) copy-start(bf16[4,4,2,7,128,128]{5,4,3,2,1,0:T(8,128)(2,1)} %get-tuple-element.12) | copy-start | bytes 22020100
  196.6 3.4 %copy-start = (f32[2048,1024]{1,0:T(8,128)S(1)}, f32[2048,1024]{1,0:T(8,128)}, u32[]{:S(2)}) copy-start(f32[2048,1024]{1,0:T(8,128)} %get-tuple-element.16.full) | copy-start | bytes 25165828
  200.0 2.2 %copy-start.3 = (bf16[2048,1024]{1,0:T(8,128)(2,1)S(1)}, bf16[2048,1024]{1,0:T(8,128)(2,1)}, u32[]{:S(2)}) copy-start(bf16[2048,1024]{1,0:T(8,128)(2,1)} %get-tuple-element.17.low) | copy-start | bytes 12582916

commit v2 on v1

v2 whole, which is shorter than its diff:
```python
import functools

import jax
import jax.numpy as jnp
from jax import lax
from jax.experimental import pallas as pl
from jax.experimental.pallas import tpu as pltpu
from jax.sharding import PartitionSpec as P

TILE = 128
PANEL = 512
SLOTS = 7
NT = 64
ROWS = 2048
COLS = 1024
MESH = pl.DeviceIdType.MESH
ANY = pl.BlockSpec(memory_space=pl.ANY)
VMEM = pl.BlockSpec(memory_space=pltpu.VMEM)
SMEM = pl.BlockSpec(memory_space=pltpu.SMEM)
HBM = pl.BlockSpec(memory_space=pltpu.HBM)
F32 = jnp.float32
BF16 = jnp.bfloat16
SCOPED = 20 << 20


def position():
    col = lax.axis_index("col")
    return lax.axis_index("front"), lax.axis_index("row"), col // 2, lax.rem(col, 2)


def mod4(v):
    return lax.rem(v + 8, 4)


def device(x, y, z, k):
    return (x, mod4(y), mod4(z) * 2 + k)


def remote(src, dst, send, recv, to):
    return pltpu.make_async_remote_copy(src, dst, send, recv, device_id=to, device_id_type=MESH)


def greet(peers):
    barrier = pltpu.get_barrier_semaphore()
    for peer in peers:
        pl.semaphore_signal(barrier, inc=1, device_id=peer, device_id_type=MESH)
    pl.semaphore_wait(barrier, len(peers))


STEPS = (1, 3, 2)


def exchange_kernel(src, own_map, front, dst, maps, acc, mid, send, recv, map_send, map_recv, local):
    x, y, z, k = position()
    other = 1 - k
    me = y * 8 + z * 2 + k

    def partner(d):
        to = lax.rem(me + d, 32)
        return x, to // 8, lax.rem(to, 8)

    greet([partner(d) for d in range(1, 32)])
    count = 0

    def send_to(block, target, to):
        nonlocal count
        copy = remote(block, target, send.at[count], recv.at[count], to)
        copy.start()
        count += 1
        return copy

    first = []
    for a in STEPS:
        for b in STEPS:
            first.append(
                (
                    send_to(src.at[mod4(y + a), mod4(z + b), k], mid.at[0, a, b], device(x, y + a, z, k)),
                    send_to(
                        src.at[mod4(y + b), mod4(z + a), other], mid.at[1, a, b], device(x, y, z + a, other)
                    ),
                    a,
                    b,
                )
            )

    def map_copy(d):
        return remote(own_map, maps.at[me], map_send.at[d], map_recv.at[d], partner(d))

    @pl.loop(1, 32)
    def _(d):
        map_copy(d).start()

    rest = []
    for d in STEPS:
        rest.append(send_to(src.at[mod4(y + d), z, k], dst.at[y, z, k], device(x, y + d, z, k)))
        rest.append(send_to(src.at[y, mod4(z + d), k], dst.at[y, z, k], device(x, y, z + d, k)))
        rest.append(send_to(src.at[mod4(y + d), z, other], dst.at[y, z, k], device(x, y + d, z, other)))
        rest.append(send_to(src.at[y, mod4(z + d), other], dst.at[y, z, k], device(x, y, z + d, other)))
    rest.append(send_to(src.at[y, z, other], dst.at[y, z, k], device(x, y, z, other)))
    own = [
        pltpu.make_async_copy(src.at[y, z, k], dst.at[y, z, k], local.at[0]),
        pltpu.make_async_copy(own_map, maps.at[me], local.at[1]),
        pltpu.make_async_copy(front, acc, local.at[2]),
    ]
    for copy in own:
        copy.start()
    for by_row, by_col, a, b in first:
        by_row.wait_recv()
        rest.append(send_to(mid.at[0, a, b], dst.at[mod4(y - a), z, k], device(x, y, z + b, k)))
        by_col.wait_recv()
        rest.append(send_to(mid.at[1, a, b], dst.at[y, mod4(z - a), other], device(x, y + b, z, k)))
    for by_row, by_col, _, _ in first:
        by_row.wait_send()
        by_col.wait_send()
    for copy in own:
        copy.wait()

    @pl.loop(1, 32)
    def _(d):
        map_copy(d).wait()

    for copy in rest:
        copy.wait()


def exchange(tiles, child_map, front):
    shape = (4, 4, 2, SLOTS, TILE, TILE)
    copies = 18 + 13 + 18
    return pl.pallas_call(
        exchange_kernel,
        out_shape=(
            pltpu.VMEM(shape, tiles.dtype),
            jax.ShapeDtypeStruct((32, *child_map.shape), child_map.dtype),
            pltpu.VMEM(front.shape, front.dtype),
            jax.ShapeDtypeStruct((2, 4, 4, SLOTS, TILE, TILE), tiles.dtype),
        ),
        in_specs=[HBM, HBM, HBM],
        out_specs=(VMEM, ANY, VMEM, HBM),
        scratch_shapes=[
            pltpu.SemaphoreType.DMA((copies,)),
            pltpu.SemaphoreType.DMA((copies,)),
            pltpu.SemaphoreType.DMA((32,)),
            pltpu.SemaphoreType.DMA((32,)),
            pltpu.SemaphoreType.DMA((3,)),
        ],
        compiler_params=pltpu.CompilerParams(
            collective_id=0, has_side_effects=True, vmem_limit_bytes=SCOPED
        ),
        name="exchange",
    )(*(pltpu.with_memory_space_constraint(v, pltpu.HBM) for v in (tiles.reshape(shape), child_map, front)))[:3]


def split(x):
    high = x.astype(BF16)
    return high, (x - high.astype(F32)).astype(BF16)


def wide_dot(a, b_high, b_low):
    a_high, a_low = split(a)
    dot = functools.partial(jnp.dot, preferred_element_type=F32)
    return dot(a_high, b_high) + (dot(a_low, b_high) + dot(a_high, b_low))


def assemble_kernel(maps, kids, front, full):
    row = lax.axis_index("row")
    col = lax.axis_index("col")
    first = (row * 8 + col) * SLOTS

    @pl.loop(0, 32)
    def _(source):
        for slot in range(SLOTS):
            t = maps[source, 0, first + slot]
            r = pl.multiple_of((t // NT - row * 16) * TILE, TILE)
            c = pl.multiple_of((lax.rem(t, NT) - col * 8) * TILE, TILE)
            full[pl.ds(r, TILE), pl.ds(c, TILE)] += kids[source * SLOTS + slot].astype(F32)


def assemble(maps, kids, front):
    return pl.pallas_call(
        assemble_kernel,
        out_shape=pltpu.VMEM((ROWS, COLS), F32),
        in_specs=[SMEM, VMEM, VMEM],
        out_specs=VMEM,
        input_output_aliases={2: 0},
        compiler_params=pltpu.CompilerParams(vmem_limit_bytes=SCOPED),
        name="assemble",
    )(maps, kids, front)


PIECES = 8
WINDOW = 3
SKEW = 2
GAP = 2 * (SKEW - 1)


def lower_chunk(way, i):
    return lax.rem(i // 2 + 1, 4) * 4 + 2 * way + lax.rem(i, 2)


def upper_chunk(way, i):
    return lax.rem(i // 4 * 4 + 4, 8) + 2 * way + lax.rem(i, 4) // 2, lax.rem(i, 2)


def rows_of(chunk, count):
    return pl.ds(pl.multiple_of(chunk * count, count), count)


def share_kernel(
    full, inverse, pattern, low, up, mat, pivot_rows,
    inv, inv_high, inv_low, send_low, recv_low, send_core, send_up, recv_up, sem
):
    x, y, z, k = position()
    first_row = y == 0
    first_col = (z == 0) & (k == 0)
    right = device(x, y, z + 1, k), device(x, y, z - 1, k)
    down = device(x, y + 1, z, k), device(x, y - 1, z, k)
    across = device(x, y, z, 1 - k)
    low_hops = z, mod4(-z)
    up_hops = y, mod4(-y)

    def kept(chunk, tile_col):
        return pattern[y * 16 + chunk, (z * 2 + k) * 8 + tile_col].astype(F32)

    seeds = first_row & jnp.logical_not(first_col)
    inv_load = pltpu.make_async_copy(inverse, inv, sem)

    @pl.when(first_col)
    def _():
        inv_load.start()

    @pl.when(first_row)
    def _():
        up[0:PANEL, :] = full[0:PANEL, :].astype(BF16)

    @pl.when(first_col)
    def _():
        inv_load.wait()
        high, rest = split(inv[...])
        inv_high[...] = high
        inv_low[...] = rest

    greet([*right, *down, across])

    def low_piece(way, g):
        panel, i = g // PIECES, lax.rem(g, PIECES)
        return low.at[rows_of(lower_chunk(way, i), TILE), pl.ds(pl.multiple_of(panel * PANEL, PANEL), PANEL)]

    def low_copy(way, g):
        n = way * 2 * PIECES + g
        piece = low_piece(way, g)
        return remote(piece, piece, send_low.at[n], recv_low.at[n], right[way])

    def core_copy(way, g):
        n = way * 2 * PIECES + g
        piece = low_piece(way, g)
        return remote(piece, piece, send_core.at[n], recv_low.at[n], across)

    def up_copy(way, g):
        n = way * 2 * PIECES + g
        panel, i = g // PIECES, lax.rem(g, PIECES)
        chunk, half = upper_chunk(way, i)
        piece = up.at[rows_of(panel * 2 + half, 256), rows_of(chunk, TILE)]
        return remote(piece, piece, send_up.at[n], recv_up.at[n], down[way])

    def make_low(g):
        i = lax.rem(g, PIECES)
        group = lower_chunk(0, i) // 4
        rows = rows_of(group, PANEL)
        solved = (y > 0) | (group >= 1)

        @pl.when(g < PIECES)
        def _():
            part = wide_dot(full[rows, 0:PANEL], inv_high[0], inv_low[0])
            low[rows, 0:PANEL] = part.astype(BF16)
            mat[rows, PANEL:] = full[rows, PANEL:]

            @pl.when(solved)
            def _():
                mat[rows, 0:PANEL] = part

            @pl.when(jnp.logical_not(solved))
            def _():
                mat[rows, 0:PANEL] = full[rows, 0:PANEL]

        @pl.when((g >= PIECES) & solved)
        def _():
            cut = jnp.dot(low[rows, 0:PANEL], up[0:PANEL, PANEL:], preferred_element_type=F32)
            for m in range(4):
                for n in range(4):
                    here = pl.ds(pl.multiple_of(group * PANEL + m * TILE, TILE), TILE)
                    cols = slice(PANEL + n * TILE, PANEL + (n + 1) * TILE)
                    mat[here, cols] -= cut[m * TILE : (m + 1) * TILE, n * TILE : (n + 1) * TILE] * kept(
                        group * 4 + m, 4 + n
                    )
            part = wide_dot(mat[rows, PANEL:], inv_high[1], inv_low[1])
            low[rows, PANEL:] = part.astype(BF16)

            @pl.when((y > 0) | (group >= 2))
            def _():
                mat[rows, PANEL:] = part

        @pl.when((g >= PIECES) & jnp.logical_not(solved))
        def _():
            low[rows, PANEL:] = jnp.zeros((PANEL, PANEL), BF16)

    def make_up(way, g):
        chunk, _ = upper_chunk(way, lax.rem(g, PIECES))
        cols = rows_of(chunk, TILE)
        cut = jnp.dot(low[PANEL : 2 * PANEL, 0:PANEL], up[0:PANEL, cols], preferred_element_type=F32)
        for n in range(4):
            tile = slice(n * TILE, (n + 1) * TILE)
            value = full[PANEL + n * TILE : PANEL + (n + 1) * TILE, cols] - cut[tile] * kept(4 + n, chunk)
            pivot_rows[tile, cols] = value
            up[PANEL + n * TILE : PANEL + (n + 1) * TILE, cols] = value.astype(BF16)

    total = 2 * PIECES

    def due(step):
        late = step >= PIECES + GAP
        return jnp.where(late, step - GAP, step), ((step >= 0) & (step < PIECES)) | (late & (step < total + GAP))

    @pl.loop(0, total + GAP + 3 * SKEW + 1)
    def _(t):
        for way in (0, 1):
            i, here = due(t - SKEW * up_hops[way])

            @pl.when(here)
            def _(way=way, i=i):
                @pl.when(y != 0)
                def _():
                    up_copy(way, i).wait_recv()

                @pl.when(first_row & (i >= PIECES) & (lax.rem(i, 2) == 0))
                def _():
                    make_up(way, i)

                @pl.when(up_hops[way] < 3)
                def _():
                    @pl.when(i >= WINDOW)
                    def _():
                        up_copy(way, i - WINDOW).wait_send()

                    up_copy(way, i).start()

        g, here = due(t)

        @pl.when(first_col & here & (lax.rem(g, 2) == 0))
        def _():
            make_low(g)

        for way in (0, 1):
            j, here = due(t - SKEW * low_hops[way] - k)

            @pl.when(here)
            def _(way=way, j=j):
                @pl.when(jnp.logical_not(first_col))
                def _():
                    low_copy(way, j).wait_recv()

                @pl.when((k == 0) & (low_hops[way] < 3))
                def _():
                    @pl.when(j >= WINDOW)
                    def _():
                        low_copy(way, j - WINDOW).wait_send()

                    low_copy(way, j).start()

                @pl.when(k == 0)
                def _():
                    @pl.when(j >= WINDOW)
                    def _():
                        core_copy(way, j - WINDOW).wait_send()

                    core_copy(way, j).start()

    for way in (0, 1):
        for i in range(total - WINDOW, total):
            @pl.when(up_hops[way] < 3)
            def _():
                up_copy(way, i).wait_send()

            @pl.when((k == 0) & (low_hops[way] < 3))
            def _():
                low_copy(way, i).wait_send()

            @pl.when(k == 0)
            def _():
                core_copy(way, i).wait_send()


def share(full, inverse, pattern):
    dma = pltpu.SemaphoreType.DMA((2 * 2 * PIECES,))
    return pl.pallas_call(
        share_kernel,
        out_shape=(
            pltpu.VMEM((ROWS, 2 * PANEL), BF16),
            pltpu.VMEM((2 * PANEL, COLS), BF16),
            pltpu.VMEM((ROWS, COLS), F32),
            pltpu.VMEM((PANEL, COLS), F32),
        ),
        in_specs=[VMEM, ANY, SMEM],
        out_specs=(VMEM, VMEM, VMEM, VMEM),
        scratch_shapes=[
            pltpu.VMEM((2, PANEL, PANEL), F32),
            pltpu.VMEM((2, PANEL, PANEL), BF16),
            pltpu.VMEM((2, PANEL, PANEL), BF16),
            dma,
            dma,
            dma,
            dma,
            dma,
            pltpu.SemaphoreType.DMA,
        ],
        compiler_params=pltpu.CompilerParams(
            collective_id=1, has_side_effects=True, vmem_limit_bytes=SCOPED
        ),
        name="share",
    )(full, inverse, pattern)


BLOCK = 512


def update_kernel(pattern, full, low, up, mat, pivot_rows, out, slots, sems):
    row = lax.axis_index("row")
    col = lax.axis_index("col")
    first_col = col == 0
    first_row = row == 0

    def store(source, block):
        return pltpu.make_async_copy(source, out.at[rows_of(block, BLOCK)], sems.at[lax.rem(block, 2)])

    @pl.when(first_col)
    def _():
        copy = pltpu.make_async_copy(mat, out, sems.at[2])
        copy.start()
        copy.wait()

    @pl.when(jnp.logical_not(first_col))
    def _():
        start = jnp.where(first_row, 2, 0)
        above = [
            pltpu.make_async_copy(full.at[0:PANEL], out.at[0:PANEL], sems.at[2]),
            pltpu.make_async_copy(pivot_rows, out.at[PANEL : 2 * PANEL], sems.at[3]),
        ]

        @pl.when(first_row)
        def _():
            for copy in above:
                copy.start()

        @pl.loop(start, ROWS // BLOCK)
        def _(block):
            rows = rows_of(block, BLOCK)
            slot = lax.rem(block, 2)

            @pl.when(block >= start + 2)
            def _():
                store(slots.at[slot], block).wait()

            cut = jnp.dot(low[rows, :], up[...], preferred_element_type=F32)
            for m in range(BLOCK // TILE):
                here = pl.ds(pl.multiple_of(block * BLOCK + m * TILE, TILE), TILE)
                tile = slice(m * TILE, (m + 1) * TILE)
                for c in range(COLS // TILE):
                    cols = slice(c * TILE, (c + 1) * TILE)
                    keep = pattern[row * 16 + block * (BLOCK // TILE) + m, col * 8 + c].astype(F32)
                    slots[slot, tile, cols] = full[here, cols] - cut[tile, cols] * keep
            store(slots.at[slot], block).start()

        for block in (2, 3):
            store(slots.at[block % 2], block).wait()

        @pl.when(first_row)
        def _():
            for copy in above:
                copy.wait()


def update(pattern, full, low, up, mat, pivot_rows):
    return pl.pallas_call(
        update_kernel,
        out_shape=jax.ShapeDtypeStruct((ROWS, COLS), F32),
        in_specs=[SMEM, VMEM, VMEM, VMEM, VMEM, VMEM],
        out_specs=ANY,
        scratch_shapes=[pltpu.VMEM((2, BLOCK, COLS), F32), pltpu.SemaphoreType.DMA((4,))],
        compiler_params=pltpu.CompilerParams(vmem_limit_bytes=SCOPED),
        name="update",
    )(pattern, full, low, up, mat, pivot_rows)


def body(front_in, child_tiles, child_map, pattern, pivot_inverse):
    kids, maps, front = exchange(child_tiles, child_map, front_in)
    full = assemble(maps, kids.reshape(-1, TILE, TILE), front)
    low, up, mat, pivot_rows = share(full, pivot_inverse, pattern)
    return update(pattern, full, low, up, mat, pivot_rows)


def solution(mesh):
    return jax.shard_map(
        body,
        mesh=mesh,
        in_specs=(
            P(("front", "row"), "col"),
            P(("front", "row", "col"), None, None, None),
            P(("front", "row", "col"), None),
            P("front", None),
            P("front", None, None),
        ),
        out_specs=P(("front", "row"), "col"),
        check_vma=False,
    )
```

time: 210 us -> 151 us (0.72)
  Pallas kernels: 188 us -> 151 us
  local copies, waits for them, and re-layouts: 10.1 us -> 0.01 us
  starting transfers between devices: 8.41 us -> 0 us
  other arithmetic: 2.95 us -> 0 us
    pallas_call x3, Pallas kernels: 181 us -> 143 us  [the longest x1 87.6 us: exchange(): pl.pallas_call(exchange_kernel, out_shape=(pltpu.VMEM(shape, tiles.dtype)...]
    unnamed x10 -> x4, local copies, waits for them, and re-layouts: 9.25 us -> 0.01 us
    all_to_all x1 -> x0, starting transfers between devices: 8.41 us -> none  [body(): lax.all_to_all(child_map.reshape(32, SLOTS), ('row', 'col'), split_axis=0...]
  transfers between devices with their start and end apart: 1 -> 0, of which waited for: 0 -> 0; matrix products, arithmetic and copies ran while one was open for 0% -> 0% of each run, Pallas kernels for 40% -> 0%
where the time goes in v2:
time: 151 us
  Pallas kernels  151 us (100%)
    pallas_call x1, Pallas kernels, exchange(): pl.pallas_call(exchange_kernel, out_shape=(pltpu.VMEM(shape, tiles.dtype)...  87.6 us
    pallas_call x1, Pallas kernels, share(): pl.pallas_call(share_kernel, out_shape=(pltpu.VMEM((ROWS, 2 * PANEL), BF1...  51.5 us
    pallas_call x1, Pallas kernels, update(): pl.pallas_call(update_kernel, out_shape=jax.ShapeDtypeStruct((ROWS, COLS)...  7.54 us
    pallas_call x1, Pallas kernels, assemble(): pl.pallas_call(assemble_kernel, out_shape=pltpu.VMEM((ROWS, COLS), F32),...  4.25 us

profile of v2, /device:TPU:47, one launch (start us, length us, event | category | flops | bytes accessed | tf_op | source)
XLA Modules:
  0.0 151.0 jit_solution(17075102998475349466)
XLA Ops:
  0.0 87.6 %exchange.1 = (bf16[4,4,2,7,128,128]{5,4,3,2,1,0:T(8,128)(2,1)S(1)}, s32[32,1,224]{2,1,0:T(1,128)S(1)}, f32[2048,1024]{1,0:T(8,128)S(1)}, bf16[2,4,4,7,128,128]{5,4,3,2,1,0:T(8,128)(2,1)}) custom-call(bf16[4,4,2,7,128,128]{5,4,3,2,1,0:T(8,128)(2,1)} %bitcast.3, s32[1,224]{1,0:T(1,128)} %own_map.1, f32[2048,1024]{1,0:T(8,128)} %front.1), custom_call_target="tpu_custom_call" | custom-call | tf_op jit(solution)/shard_map/exchange/pallas_call | solution.py:129
  87.6 0.0 copy-start
  87.7 0.0 copy-start.1
  87.7 4.3 %assemble.1.full = f32[2048,1024]{1,0:T(8,128)S(1)} custom-call(s32[32,1,224]{2,1,0:T(1,128)S(1)} %get-tuple-element.12.maps, bf16[224,128,128]{2,1,0:T(8,128)(2,1)S(1)} %bitcast.2, f32[2048,1024]{1,0:T(8,128)S(1)} %get-tuple-element.14.front), custom_call_target="tpu_custom_call", output_to_operand_aliasing={{}: (2, {})} | custom-call | tf_op jit(solution)/shard_map/assemble/pallas_call | solution.py:179
  91.9 0.0 copy-done
  91.9 0.0 copy-done.1
  91.9 51.5 %share.1 = (bf16[2048,1024]{1,0:T(8,128)(2,1)S(1)}, bf16[1024,1024]{1,0:T(8,128)(2,1)S(1)}, f32[2048,1024]{1,0:T(8,128)S(1)}, f32[512,1024]{1,0:T(8,128)S(1)}) custom-call(f32[2048,1024]{1,0:T(8,128)S(1)} %assemble.1.full, f32[2,512,512]{2,1,0:T(8,128)S(1)} %copy-done, s32[64,64]{1,0:T(8,128)S(1)} %copy-done.1), custom_call_target="tpu_custom_call" | custom-call | tf_op jit(solution)/shard_map/share/pallas_call | solution.py:393
  143.4 7.5 %update.1 = f32[2048,1024]{1,0:T(8,128)} custom-call(s32[64,64]{1,0:T(8,128)S(1)} %copy-done.1, f32[2048,1024]{1,0:T(8,128)S(1)} %assemble.1.full, bf16[2048,1024]{1,0:T(8,128)(2,1)S(1)} %get-tuple-element.15.low, bf16[1024,1024]{1,0:T(8,128)(2,1)S(1)} %get-tuple-element.16.up, f32[2048,1024]{1,0:T(8,128)S(1)} %get-tuple-element.17.mat, ...), custom_call_target="tpu_custom_call" | custom-call | tf_op jit(solution)/shard_map/update/pallas_call | solution.py:481
Async XLA Ops:
  87.6 4.3 %copy-start = (f32[2,512,512]{2,1,0:T(8,128)S(1)}, f32[2,512,512]{2,1,0:T(8,128)}, u32[]{:S(2)}) copy-start(f32[2,512,512]{2,1,0:T(8,128)} %inverse.1) | copy-start | bytes 6291460
  87.7 4.3 %copy-start.1 = (s32[64,64]{1,0:T(8,128)S(1)}, s32[64,64]{1,0:T(8,128)}, u32[]{:S(2)}) copy-start(s32[64,64]{1,0:T(8,128)} %pattern.3) | copy-start | bytes 49156

commit v3 on v2

--- a/solution.py
+++ b/solution.py
@@ -20,7 +20,7 @@
 HBM = pl.BlockSpec(memory_space=pltpu.HBM)
 F32 = jnp.float32
 BF16 = jnp.bfloat16
-SCOPED = 20 << 20
+SCOPED = 16 << 20
 
 
 def position():
@@ -48,6 +48,7 @@
 
 
 STEPS = (1, 3, 2)
+TURNS = ((1, 3), (3, 1), (2, 2), (3, 3), (1, 1), (2, 1), (1, 2), (3, 2), (2, 3))
 
 
 def exchange_kernel(src, own_map, front, dst, maps, acc, mid, send, recv, map_send, map_recv, local):
@@ -70,18 +71,15 @@
         return copy
 
     first = []
-    for a in STEPS:
-        for b in STEPS:
-            first.append(
-                (
-                    send_to(src.at[mod4(y + a), mod4(z + b), k], mid.at[0, a, b], device(x, y + a, z, k)),
-                    send_to(
-                        src.at[mod4(y + b), mod4(z + a), other], mid.at[1, a, b], device(x, y, z + a, other)
-                    ),
-                    a,
-                    b,
-                )
+    for a, b in TURNS:
+        first.append(
+            (
+                send_to(src.at[mod4(y + a), mod4(z + b), k], mid.at[0, a, b], device(x, y + a, z, k)),
+                send_to(src.at[mod4(y + b), mod4(z + a), other], mid.at[1, a, b], device(x, y, z + a, other)),
+                a,
+                b,
             )
+        )
 
     def map_copy(d):
         return remote(own_map, maps.at[me], map_send.at[d], map_recv.at[d], partner(d))
@@ -187,34 +185,37 @@
     )(maps, kids, front)
 
 
-PIECES = 8
+PART = 2
+PIECES = 4 * PART
 WINDOW = 3
-SKEW = 2
-GAP = 2 * (SKEW - 1)
-
-
-def lower_chunk(way, i):
-    return lax.rem(i // 2 + 1, 4) * 4 + 2 * way + lax.rem(i, 2)
-
-
-def upper_chunk(way, i):
-    return lax.rem(i // 4 * 4 + 4, 8) + 2 * way + lax.rem(i, 4) // 2, lax.rem(i, 2)
+SKEW = 3
+LEAD = 2
+GAP = max(0, 3 * SKEW + LEAD + PART - 1 - PIECES)
 
 
 def rows_of(chunk, count):
     return pl.ds(pl.multiple_of(chunk * count, count), count)
 
 
+def lower_group(i):
+    return lax.rem(i // PART + 1, 4)
+
+
+def upper_chunk(way, i):
+    q = i // PART
+    return lax.rem(q // 2 * 4 + 4, 8) + 2 * way + lax.rem(q, 2)
+
+
 def share_kernel(
     full, inverse, pattern, low, up, mat, pivot_rows,
-    inv, inv_high, inv_low, send_low, recv_low, send_core, send_up, recv_up, sem
+    inv, inv_high, inv_low, send_low, recv_low, send_core, send_up, recv_up, send_corner, recv_corner, sem
 ):
     x, y, z, k = position()
     first_row = y == 0
     first_col = (z == 0) & (k == 0)
-    right = device(x, y, z + 1, k), device(x, y, z - 1, k)
     down = device(x, y + 1, z, k), device(x, y - 1, z, k)
     across = device(x, y, z, 1 - k)
+    ahead = device(x, y, z + 1, 0), device(x, y, z - 1, 1)
     low_hops = z, mod4(-z)
     up_hops = y, mod4(-y)
 
@@ -239,16 +240,20 @@
         inv_high[...] = high
         inv_low[...] = rest
 
-    greet([*right, *down, across])
+    greet(
+        [device(x, y, z + d, c) for d in (1, -1) for c in (k, 1 - k)]
+        + [*down, across]
+    )
 
     def low_piece(way, g):
         panel, i = g // PIECES, lax.rem(g, PIECES)
-        return low.at[rows_of(lower_chunk(way, i), TILE), pl.ds(pl.multiple_of(panel * PANEL, PANEL), PANEL)]
+        row = (lower_group(i) * 2 + way) * PART + lax.rem(i, PART)
+        return low.at[rows_of(row, 256 // PART), rows_of(panel, PANEL)]
 
     def low_copy(way, g):
         n = way * 2 * PIECES + g
         piece = low_piece(way, g)
-        return remote(piece, piece, send_low.at[n], recv_low.at[n], right[way])
+        return remote(piece, piece, send_low.at[n], recv_low.at[n], ahead[way])
 
     def core_copy(way, g):
         n = way * 2 * PIECES + g
@@ -258,13 +263,13 @@
     def up_copy(way, g):
         n = way * 2 * PIECES + g
         panel, i = g // PIECES, lax.rem(g, PIECES)
-        chunk, half = upper_chunk(way, i)
-        piece = up.at[rows_of(panel * 2 + half, 256), rows_of(chunk, TILE)]
+        piece = up.at[
+            rows_of(panel * PART + lax.rem(i, PART), PANEL // PART), rows_of(upper_chunk(way, i), TILE)
+        ]
         return remote(piece, piece, send_up.at[n], recv_up.at[n], down[way])
 
     def make_low(g):
-        i = lax.rem(g, PIECES)
-        group = lower_chunk(0, i) // 4
+        group = lower_group(lax.rem(g, PIECES))
         rows = rows_of(group, PANEL)
         solved = (y > 0) | (group >= 1)
 
@@ -304,7 +309,7 @@
             low[rows, PANEL:] = jnp.zeros((PANEL, PANEL), BF16)
 
     def make_up(way, g):
-        chunk, _ = upper_chunk(way, lax.rem(g, PIECES))
+        chunk = upper_chunk(way, lax.rem(g, PIECES))
         cols = rows_of(chunk, TILE)
         cut = jnp.dot(low[PANEL : 2 * PANEL, 0:PANEL], up[0:PANEL, cols], preferred_element_type=F32)
         for n in range(4):
@@ -313,79 +318,155 @@
             pivot_rows[tile, cols] = value
             up[PANEL + n * TILE : PANEL + (n + 1) * TILE, cols] = value.astype(BF16)
 
+    def corner_copy(n, d):
+        piece = up.at[rows_of(n, TILE), pl.ds(PANEL, PANEL)]
+        slot = n if d > 0 else 4 + n
+        return remote(piece, piece, send_corner.at[slot], recv_corner.at[n], device(x, y + d, z, k))
+
+    def pass_corner(n):
+        for d in (1, -1):
+            @pl.when(y == mod4(d))
+            def _(d=d):
+                copy = corner_copy(n if d > 0 else 2 + n, d)
+                copy.wait_recv()
+                copy.start()
+
+    @pl.when(first_row & first_col)
+    def _():
+        for n in range(2):
+            for d, piece in ((1, n), (-1, 2 + n)):
+                corner_copy(piece, d).start()
+        for n in range(2):
+            for d, piece in ((1, 2 + n), (-1, n)):
+                corner_copy(piece, d).start()
+
     total = 2 * PIECES
 
     def due(step):
-        late = step >= PIECES + GAP
-        return jnp.where(late, step - GAP, step), ((step >= 0) & (step < PIECES)) | (late & (step < total + GAP))
-
-    @pl.loop(0, total + GAP + 3 * SKEW + 1)
+        second = step >= PIECES + GAP
+        return jnp.where(second, step - GAP, step), ((step >= 0) & (step < PIECES)) | (second & (step < total + GAP))
+
+    def paced(copy_of, way, g):
+        @pl.when(g >= WINDOW)
+        def _():
+            copy_of(way, g - WINDOW).wait_send()
+
+        copy_of(way, g).start()
+
+    def drain(copy_of, way):
+        @pl.loop(total - WINDOW, total)
+        def _(g):
+            copy_of(way, g).wait_send()
+
+    def arrivals(copy_of, way, start, stop):
+        @pl.loop(start, stop)
+        def _(g):
+            copy_of(way, g).wait_recv()
+
+    def hold_low(way):
+        return (z != 0) & (k == way)
+
+    @pl.loop(0, total + GAP + 3 * SKEW + LEAD)
     def _(t):
         for way in (0, 1):
-            i, here = due(t - SKEW * up_hops[way])
-
-            @pl.when(here)
+            j, here = due(t - SKEW * low_hops[way] - LEAD)
+
+            @pl.when(here & hold_low(way))
+            def _(way=way, j=j):
+                low_copy(way, j).wait_recv()
+
+                @pl.when(low_hops[way] < 3)
+                def _():
+                    paced(low_copy, way, j)
+
+                paced(core_copy, way, j)
+
+        for way in (0, 1):
+            i, here = due(t - SKEW * up_hops[way] - LEAD)
+
+            @pl.when(here & (y != 0) & (up_hops[way] < 3) & jnp.logical_not(first_col))
             def _(way=way, i=i):
-                @pl.when(y != 0)
-                def _():
-                    up_copy(way, i).wait_recv()
-
-                @pl.when(first_row & (i >= PIECES) & (lax.rem(i, 2) == 0))
-                def _():
-                    make_up(way, i)
-
-                @pl.when(up_hops[way] < 3)
-                def _():
-                    @pl.when(i >= WINDOW)
-                    def _():
-                        up_copy(way, i - WINDOW).wait_send()
-
-                    up_copy(way, i).start()
+                up_copy(way, i).wait_recv()
+                paced(up_copy, way, i)
 
         g, here = due(t)
 
-        @pl.when(first_col & here & (lax.rem(g, 2) == 0))
-        def _():
-            make_low(g)
-
-        for way in (0, 1):
-            j, here = due(t - SKEW * low_hops[way] - k)
-
-            @pl.when(here)
-            def _(way=way, j=j):
-                @pl.when(jnp.logical_not(first_col))
-                def _():
-                    low_copy(way, j).wait_recv()
-
-                @pl.when((k == 0) & (low_hops[way] < 3))
-                def _():
-                    @pl.when(j >= WINDOW)
-                    def _():
-                        low_copy(way, j - WINDOW).wait_send()
-
-                    low_copy(way, j).start()
-
-                @pl.when(k == 0)
-                def _():
-                    @pl.when(j >= WINDOW)
-                    def _():
-                        core_copy(way, j - WINDOW).wait_send()
-
-                    core_copy(way, j).start()
+        @pl.when(here & seeds)
+        def _():
+            @pl.when(g == PIECES)
+            def _():
+                for way in (0, 1):
+                    @pl.when(jnp.logical_not(hold_low(way)))
+                    def _(way=way):
+                        arrivals(low_copy, way, 0, PART)
+
+            for way in (0, 1):
+                @pl.when((g >= PIECES) & (lax.rem(g, PART) == 0))
+                def _(way=way):
+                    make_up(way, g)
+
+                paced(up_copy, way, g)
+
+        @pl.when(here & first_col)
+        def _():
+            @pl.when(t == 4)
+            def _():
+                pass_corner(0)
+
+            @pl.when(t == 6)
+            def _():
+                pass_corner(1)
+
+            @pl.when(g == PIECES)
+            def _():
+                for n in range(4):
+                    @pl.when((y == 2) | ((y == 1) & (n >= 2)) | ((y == 3) & (n < 2)))
+                    def _(n=n):
+                        corner_copy(n, 1).wait_recv()
+
+            @pl.when(lax.rem(g, PART) == 0)
+            def _():
+                make_low(g)
+
+            for way in (0, 1):
+                paced(low_copy, way, g)
+                paced(core_copy, way, g)
+
+    @pl.when(first_col)
+    def _():
+        for n in range(4):
+            @pl.when(first_row | ((y == 1) & (n < 2)))
+            def _(n=n):
+                corner_copy(n, 1).wait_send()
+
+            @pl.when(first_row | ((y == 3) & (n >= 2)))
+            def _(n=n):
+                corner_copy(n, -1).wait_send()
 
     for way in (0, 1):
-        for i in range(total - WINDOW, total):
-            @pl.when(up_hops[way] < 3)
-            def _():
-                up_copy(way, i).wait_send()
-
-            @pl.when((k == 0) & (low_hops[way] < 3))
-            def _():
-                low_copy(way, i).wait_send()
-
-            @pl.when(k == 0)
-            def _():
-                core_copy(way, i).wait_send()
+        @pl.when(jnp.logical_not(first_col | hold_low(way)))
+        def _(way=way):
+            @pl.when(jnp.logical_not(first_row))
+            def _():
+                arrivals(low_copy, way, 0, PART)
+
+            arrivals(low_copy, way, PART, total)
+
+        @pl.when((y != 0) & (up_hops[way] == 3) & jnp.logical_not(first_col))
+        def _(way=way):
+            arrivals(up_copy, way, 0, total)
+
+        @pl.when((up_hops[way] < 3) & jnp.logical_not(first_col))
+        def _(way=way):
+            drain(up_copy, way)
+
+        @pl.when(first_col | (hold_low(way) & (low_hops[way] < 3)))
+        def _(way=way):
+            drain(low_copy, way)
+
+        @pl.when(first_col | hold_low(way))
+        def _(way=way):
+            drain(core_copy, way)
 
 
 def share(full, inverse, pattern):
@@ -409,6 +490,8 @@
             dma,
             dma,
             dma,
+            pltpu.SemaphoreType.DMA((8,)),
+            pltpu.SemaphoreType.DMA((4,)),
             pltpu.SemaphoreType.DMA,
         ],
         compiler_params=pltpu.CompilerParams(

time: 151 us -> 143 us (0.947)
  Pallas kernels: 151 us -> 142 us
    pallas_call x1, Pallas kernels: 51.5 us -> 43.7 us  [share(): pl.pallas_call(share_kernel, out_shape=(pltpu.VMEM((ROWS, 2 * PANEL), BF1...]
where the time goes in v3:
time: 143 us; the launch traced here: 142 us
  Pallas kernels  142 us (99%)
    pallas_call x1, Pallas kernels, exchange(): pl.pallas_call(exchange_kernel, out_shape=(pltpu.VMEM(shape, tiles.dtype)...  86.9 us
    pallas_call x1, Pallas kernels, share(): pl.pallas_call(share_kernel, out_shape=(pltpu.VMEM((ROWS, 2 * PANEL), BF1...  43.7 us
    pallas_call x1, Pallas kernels, update(): pl.pallas_call(update_kernel, out_shape=jax.ShapeDtypeStruct((ROWS, COLS)...  7.54 us
    pallas_call x1, Pallas kernels, assemble(): pl.pallas_call(assemble_kernel, out_shape=pltpu.VMEM((ROWS, COLS), F32),...  4.27 us

profile of v3, /device:TPU:47, one launch (start us, length us, event | category | flops | bytes accessed | tf_op | source)
XLA Modules:
  0.0 142.4 jit_solution(12130514997858628415)
XLA Ops:
  0.0 86.9 %exchange.1 = (bf16[4,4,2,7,128,128]{5,4,3,2,1,0:T(8,128)(2,1)S(1)}, s32[32,1,224]{2,1,0:T(1,128)S(1)}, f32[2048,1024]{1,0:T(8,128)S(1)}, bf16[2,4,4,7,128,128]{5,4,3,2,1,0:T(8,128)(2,1)}) custom-call(bf16[4,4,2,7,128,128]{5,4,3,2,1,0:T(8,128)(2,1)} %bitcast.3, s32[1,224]{1,0:T(1,128)} %own_map.1, f32[2048,1024]{1,0:T(8,128)} %front.1), custom_call_target="tpu_custom_call" | custom-call | tf_op jit(solution)/shard_map/exchange/pallas_call | solution.py:127
  86.9 0.0 copy-start
  86.9 0.0 copy-start.1
  86.9 4.3 %assemble.1.full = f32[2048,1024]{1,0:T(8,128)S(1)} custom-call(s32[32,1,224]{2,1,0:T(1,128)S(1)} %get-tuple-element.12.maps, bf16[224,128,128]{2,1,0:T(8,128)(2,1)S(1)} %bitcast.2, f32[2048,1024]{1,0:T(8,128)S(1)} %get-tuple-element.14.front), custom_call_target="tpu_custom_call", output_to_operand_aliasing={{}: (2, {})} | custom-call | tf_op jit(solution)/shard_map/assemble/pallas_call | solution.py:177
  91.2 0.0 copy-done
  91.2 0.0 copy-done.1
  91.2 43.7 %share.1 = (bf16[2048,1024]{1,0:T(8,128)(2,1)S(1)}, bf16[1024,1024]{1,0:T(8,128)(2,1)S(1)}, f32[2048,1024]{1,0:T(8,128)S(1)}, f32[512,1024]{1,0:T(8,128)S(1)}) custom-call(f32[2048,1024]{1,0:T(8,128)S(1)} %assemble.1.full, f32[2,512,512]{2,1,0:T(8,128)S(1)} %copy-done, s32[64,64]{1,0:T(8,128)S(1)} %copy-done.1), custom_call_target="tpu_custom_call" | custom-call | tf_op jit(solution)/shard_map/share/pallas_call | solution.py:474
  134.9 7.5 %update.1 = f32[2048,1024]{1,0:T(8,128)} custom-call(s32[64,64]{1,0:T(8,128)S(1)} %copy-done.1, f32[2048,1024]{1,0:T(8,128)S(1)} %assemble.1.full, bf16[2048,1024]{1,0:T(8,128)(2,1)S(1)} %get-tuple-element.15.low, bf16[1024,1024]{1,0:T(8,128)(2,1)S(1)} %get-tuple-element.16.up, f32[2048,1024]{1,0:T(8,128)S(1)} %get-tuple-element.17.mat, ...), custom_call_target="tpu_custom_call" | custom-call | tf_op jit(solution)/shard_map/update/pallas_call | solution.py:564
Async XLA Ops:
  86.9 4.3 %copy-start = (f32[2,512,512]{2,1,0:T(8,128)S(1)}, f32[2,512,512]{2,1,0:T(8,128)}, u32[]{:S(2)}) copy-start(f32[2,512,512]{2,1,0:T(8,128)} %inverse.1) | copy-start | bytes 6291460
  86.9 4.3 %copy-start.1 = (s32[64,64]{1,0:T(8,128)S(1)}, s32[64,64]{1,0:T(8,128)}, u32[]{:S(2)}) copy-start(s32[64,64]{1,0:T(8,128)} %pattern.3) | copy-start | bytes 49156

commit v4 on v3

--- a/solution.py
+++ b/solution.py
@@ -40,11 +40,14 @@
     return pltpu.make_async_remote_copy(src, dst, send, recv, device_id=to, device_id_type=MESH)
 
 
+def hail(peers):
+    for peer in peers:
+        pl.semaphore_signal(pltpu.get_barrier_semaphore(), inc=1, device_id=peer, device_id_type=MESH)
+    return len(peers)
+
+
 def greet(peers):
-    barrier = pltpu.get_barrier_semaphore()
-    for peer in peers:
-        pl.semaphore_signal(barrier, inc=1, device_id=peer, device_id_type=MESH)
-    pl.semaphore_wait(barrier, len(peers))
+    pl.semaphore_wait(pltpu.get_barrier_semaphore(), hail(peers))
 
 
 STEPS = (1, 3, 2)
@@ -188,9 +191,11 @@
 PART = 2
 PIECES = 4 * PART
 WINDOW = 3
-SKEW = 3
+SKEW = 2
 LEAD = 2
-GAP = max(0, 3 * SKEW + LEAD + PART - 1 - PIECES)
+GAP = max(0, 2 * SKEW + LEAD + PART - 1 - PIECES)
+
+UPDATE_AT = PIECES + 3 * SKEW + LEAD
 
 
 def rows_of(chunk, count):
@@ -208,7 +213,7 @@
 
 def share_kernel(
     full, inverse, pattern, low, up, mat, pivot_rows,
-    inv, inv_high, inv_low, send_low, recv_low, send_core, send_up, recv_up, send_corner, recv_corner, sem
+    inv_high, inv_low, send_low, recv_low, send_core, send_up, recv_up, send_corner, recv_corner, send_again
 ):
     x, y, z, k = position()
     first_row = y == 0
@@ -223,51 +228,6 @@
         return pattern[y * 16 + chunk, (z * 2 + k) * 8 + tile_col].astype(F32)
 
     seeds = first_row & jnp.logical_not(first_col)
-    inv_load = pltpu.make_async_copy(inverse, inv, sem)
-
-    @pl.when(first_col)
-    def _():
-        inv_load.start()
-
-    @pl.when(first_row)
-    def _():
-        up[0:PANEL, :] = full[0:PANEL, :].astype(BF16)
-
-    @pl.when(first_col)
-    def _():
-        inv_load.wait()
-        high, rest = split(inv[...])
-        inv_high[...] = high
-        inv_low[...] = rest
-
-    greet(
-        [device(x, y, z + d, c) for d in (1, -1) for c in (k, 1 - k)]
-        + [*down, across]
-    )
-
-    def low_piece(way, g):
-        panel, i = g // PIECES, lax.rem(g, PIECES)
-        row = (lower_group(i) * 2 + way) * PART + lax.rem(i, PART)
-        return low.at[rows_of(row, 256 // PART), rows_of(panel, PANEL)]
-
-    def low_copy(way, g):
-        n = way * 2 * PIECES + g
-        piece = low_piece(way, g)
-        return remote(piece, piece, send_low.at[n], recv_low.at[n], ahead[way])
-
-    def core_copy(way, g):
-        n = way * 2 * PIECES + g
-        piece = low_piece(way, g)
-        return remote(piece, piece, send_core.at[n], recv_low.at[n], across)
-
-    def up_copy(way, g):
-        n = way * 2 * PIECES + g
-        panel, i = g // PIECES, lax.rem(g, PIECES)
-        piece = up.at[
-            rows_of(panel * PART + lax.rem(i, PART), PANEL // PART), rows_of(upper_chunk(way, i), TILE)
-        ]
-        return remote(piece, piece, send_up.at[n], recv_up.at[n], down[way])
-
     def make_low(g):
         group = lower_group(lax.rem(g, PIECES))
         rows = rows_of(group, PANEL)
@@ -308,6 +268,52 @@
         def _():
             low[rows, PANEL:] = jnp.zeros((PANEL, PANEL), BF16)
 
+    peers = hail([device(x, y, z + d, c) for d in (1, -1) for c in (k, 1 - k)] + [*down, across])
+
+    def split_inverse(panel):
+        high, rest = split(inverse[panel])
+        inv_high[panel] = high
+        inv_low[panel] = rest
+
+    @pl.when(first_row)
+    def _():
+        up[0:PANEL, :] = full[0:PANEL, :].astype(BF16)
+
+    @pl.when(first_col)
+    def _():
+        split_inverse(0)
+        make_low(0)
+
+    pl.semaphore_wait(pltpu.get_barrier_semaphore(), peers)
+
+    def low_piece(way, g):
+        panel, i = g // PIECES, lax.rem(g, PIECES)
+        row = (lower_group(i) * 2 + way) * PART + lax.rem(i, PART)
+        return low.at[rows_of(row, 256 // PART), rows_of(panel, PANEL)]
+
+    def low_copy(way, g):
+        n = way * 2 * PIECES + g
+        piece = low_piece(way, g)
+        return remote(piece, piece, send_low.at[n], recv_low.at[n], ahead[way])
+
+    def again(way, g):
+        piece = low_piece(way, g)
+        to = device(x, y, z - 1 + 2 * way, way)
+        return remote(piece, piece, send_again.at[way * PART + g], recv_low.at[way * 2 * PIECES + g], to)
+
+    def core_copy(way, g):
+        n = way * 2 * PIECES + g
+        piece = low_piece(way, g)
+        return remote(piece, piece, send_core.at[n], recv_low.at[n], across)
+
+    def up_copy(way, g):
+        n = way * 2 * PIECES + g
+        panel, i = g // PIECES, lax.rem(g, PIECES)
+        piece = up.at[
+            rows_of(panel * PART + lax.rem(i, PART), PANEL // PART), rows_of(upper_chunk(way, i), TILE)
+        ]
+        return remote(piece, piece, send_up.at[n], recv_up.at[n], down[way])
+
     def make_up(way, g):
         chunk = upper_chunk(way, lax.rem(g, PIECES))
         cols = rows_of(chunk, TILE)
@@ -346,8 +352,8 @@
         second = step >= PIECES + GAP
         return jnp.where(second, step - GAP, step), ((step >= 0) & (step < PIECES)) | (second & (step < total + GAP))
 
-    def paced(copy_of, way, g):
-        @pl.when(g >= WINDOW)
+    def paced(copy_of, way, g, unsent=0):
+        @pl.when(g >= WINDOW + unsent)
         def _():
             copy_of(way, g - WINDOW).wait_send()
 
@@ -366,20 +372,65 @@
     def hold_low(way):
         return (z != 0) & (k == way)
 
+    def rest_of_first():
+        for way in (0, 1):
+            @pl.when(jnp.logical_not(hold_low(way)))
+            def _(way=way):
+                @pl.when(jnp.logical_not(first_row))
+                def _():
+                    arrivals(low_copy, way, 0, PART)
+
+                arrivals(low_copy, way, PART, PIECES)
+
+            @pl.when((y != 0) & (up_hops[way] == 3))
+            def _(way=way):
+                arrivals(up_copy, way, 0, PIECES)
+
+    def first_update(block):
+        cut = jnp.dot(low[rows_of(block, 256), 0:PANEL], up[0:PANEL, :], preferred_element_type=F32)
+        for m in range(2):
+            here = rows_of(2 * block + m, TILE)
+            for c in range(COLS // TILE):
+                cols = slice(c * TILE, (c + 1) * TILE)
+                mat[here, cols] = full[here, cols] - cut[m * TILE : (m + 1) * TILE, cols] * kept(2 * block + m, c)
+
     @pl.loop(0, total + GAP + 3 * SKEW + LEAD)
     def _(t):
+        @pl.when(jnp.logical_not(first_col) & (t >= UPDATE_AT))
+        def _():
+            @pl.when(t == UPDATE_AT)
+            def _():
+                rest_of_first()
+
+            block = t - UPDATE_AT
+
+            @pl.when((block < ROWS // 256) & ((y > 0) | (block >= 4)))
+            def _():
+                first_update(block)
+
         for way in (0, 1):
             j, here = due(t - SKEW * low_hops[way] - LEAD)
 
             @pl.when(here & hold_low(way))
             def _(way=way, j=j):
-                low_copy(way, j).wait_recv()
-
-                @pl.when(low_hops[way] < 3)
+                unsent = jnp.where(first_row & (low_hops[way] == 2), PART, 0)
+
+                @pl.when(jnp.logical_not(first_row & (low_hops[way] == 3) & (j < PART)))
                 def _():
-                    paced(low_copy, way, j)
-
-                paced(core_copy, way, j)
+                    low_copy(way, j).wait_recv()
+
+                    @pl.when((low_hops[way] < 3) & (j >= unsent))
+                    def _():
+                        paced(low_copy, way, j, unsent)
+
+                    paced(core_copy, way, j)
+
+            early = t - SKEW - LEAD
+
+            @pl.when(first_row & hold_low(way) & (low_hops[way] == 3) & (early >= 0) & (early < PART))
+            def _(way=way, early=early):
+                low_copy(way, early).wait_recv()
+                core_copy(way, early).start()
 
         for way in (0, 1):
             i, here = due(t - SKEW * up_hops[way] - LEAD)
@@ -424,13 +475,28 @@
                     def _(n=n):
                         corner_copy(n, 1).wait_recv()
 
-            @pl.when(lax.rem(g, PART) == 0)
+            @pl.when(g == PIECES)
+            def _():
+                split_inverse(1)
+
+            @pl.when((g > 0) & (lax.rem(g, PART) == 0))
             def _():
                 make_low(g)
 
             for way in (0, 1):
                 paced(low_copy, way, g)
+
+                @pl.when(first_row & (g < PART))
+                def _(way=way):
+                    again(way, g).start()
+
                 paced(core_copy, way, g)
+
+    @pl.when(first_row & first_col)
+    def _():
+        for way in (0, 1):
+            for g in range(PART):
+                again(way, g).wait_send()
 
     @pl.when(first_col)
     def _():
@@ -446,15 +512,11 @@
     for way in (0, 1):
         @pl.when(jnp.logical_not(first_col | hold_low(way)))
         def _(way=way):
-            @pl.when(jnp.logical_not(first_row))
-            def _():
-                arrivals(low_copy, way, 0, PART)
-
-            arrivals(low_copy, way, PART, total)
+            arrivals(low_copy, way, PIECES, total)
 
         @pl.when((y != 0) & (up_hops[way] == 3) & jnp.logical_not(first_col))
         def _(way=way):
-            arrivals(up_copy, way, 0, total)
+            arrivals(up_copy, way, PIECES, total)
 
         @pl.when((up_hops[way] < 3) & jnp.logical_not(first_col))
         def _(way=way):
@@ -479,10 +541,9 @@
             pltpu.VMEM((ROWS, COLS), F32),
             pltpu.VMEM((PANEL, COLS), F32),
         ),
-        in_specs=[VMEM, ANY, SMEM],
+        in_specs=[VMEM, VMEM, SMEM],
         out_specs=(VMEM, VMEM, VMEM, VMEM),
         scratch_shapes=[
-            pltpu.VMEM((2, PANEL, PANEL), F32),
             pltpu.VMEM((2, PANEL, PANEL), BF16),
             pltpu.VMEM((2, PANEL, PANEL), BF16),
             dma,
@@ -492,7 +553,7 @@
             dma,
             pltpu.SemaphoreType.DMA((8,)),
             pltpu.SemaphoreType.DMA((4,)),
-            pltpu.SemaphoreType.DMA,
+            pltpu.SemaphoreType.DMA((2 * PART,)),
         ],
         compiler_params=pltpu.CompilerParams(
             collective_id=1, has_side_effects=True, vmem_limit_bytes=SCOPED
@@ -501,7 +562,8 @@
     )(full, inverse, pattern)
 
 
-BLOCK = 512
+BLOCK = 256
+HALF = ROWS // 2
 
 
 def update_kernel(pattern, full, low, up, mat, pivot_rows, out, slots, sems):
@@ -510,21 +572,24 @@
     first_col = col == 0
     first_row = row == 0
 
-    def store(source, block):
-        return pltpu.make_async_copy(source, out.at[rows_of(block, BLOCK)], sems.at[lax.rem(block, 2)])
+    def store(block, half):
+        slot = lax.rem(block, 2)
+        rows = pl.ds(half * HALF, HALF)
+        return pltpu.make_async_copy(
+            slots.at[slot, rows], out.at[rows, rows_of(block, BLOCK)], sems.at[2 * slot + half]
+        )
 
     @pl.when(first_col)
     def _():
-        copy = pltpu.make_async_copy(mat, out, sems.at[2])
+        copy = pltpu.make_async_copy(mat, out, sems.at[4])
         copy.start()
         copy.wait()
 
     @pl.when(jnp.logical_not(first_col))
     def _():
-        start = jnp.where(first_row, 2, 0)
         above = [
-            pltpu.make_async_copy(full.at[0:PANEL], out.at[0:PANEL], sems.at[2]),
-            pltpu.make_async_copy(pivot_rows, out.at[PANEL : 2 * PANEL], sems.at[3]),
+            pltpu.make_async_copy(full.at[0:PANEL], out.at[0:PANEL], sems.at[4]),
+            pltpu.make_async_copy(pivot_rows, out.at[PANEL : 2 * PANEL], sems.at[5]),
         ]
 
         @pl.when(first_row)
@@ -532,27 +597,37 @@
             for copy in above:
                 copy.start()
 
-        @pl.loop(start, ROWS // BLOCK)
+        @pl.loop(0, COLS // BLOCK)
         def _(block):
-            rows = rows_of(block, BLOCK)
             slot = lax.rem(block, 2)
-
-            @pl.when(block >= start + 2)
-            def _():
-                store(slots.at[slot], block).wait()
-
-            cut = jnp.dot(low[rows, :], up[...], preferred_element_type=F32)
-            for m in range(BLOCK // TILE):
-                here = pl.ds(pl.multiple_of(block * BLOCK + m * TILE, TILE), TILE)
-                tile = slice(m * TILE, (m + 1) * TILE)
-                for c in range(COLS // TILE):
-                    cols = slice(c * TILE, (c + 1) * TILE)
-                    keep = pattern[row * 16 + block * (BLOCK // TILE) + m, col * 8 + c].astype(F32)
-                    slots[slot, tile, cols] = full[here, cols] - cut[tile, cols] * keep
-            store(slots.at[slot], block).start()
+            cols = rows_of(block, BLOCK)
+            for half in (0, 1):
+                @pl.when((row > 0) | (half == 1))
+                def _(half=half):
+                    @pl.when(block >= 2)
+                    def _():
+                        store(block, half).wait()
+
+                    cut = jnp.dot(
+                        low[half * HALF : (half + 1) * HALF, PANEL:], up[PANEL:, cols], preferred_element_type=F32
+                    )
+                    for m in range(HALF // TILE):
+                        tile = slice(m * TILE, (m + 1) * TILE)
+                        here = slice(half * HALF + m * TILE, half * HALF + (m + 1) * TILE)
+                        for c in range(BLOCK // TILE):
+                            part = slice(c * TILE, (c + 1) * TILE)
+                            keep = pattern[
+                                row * 16 + half * (HALF // TILE) + m, col * 8 + block * (BLOCK // TILE) + c
+                            ].astype(F32)
+                            place = rows_of(block * (BLOCK // TILE) + c, TILE)
+                            slots[slot, here, part] = mat[here, place] - cut[tile, part] * keep
+                    store(block, half).start()
 
         for block in (2, 3):
-            store(slots.at[block % 2], block).wait()
+            for half in (0, 1):
+                @pl.when((row > 0) | (half == 1))
+                def _(block=block, half=half):
+                    store(block, half).wait()
 
         @pl.when(first_row)
         def _():
@@ -566,7 +641,7 @@
         out_shape=jax.ShapeDtypeStruct((ROWS, COLS), F32),
         in_specs=[SMEM, VMEM, VMEM, VMEM, VMEM, VMEM],
         out_specs=ANY,
-        scratch_shapes=[pltpu.VMEM((2, BLOCK, COLS), F32), pltpu.SemaphoreType.DMA((4,))],
+        scratch_shapes=[pltpu.VMEM((2, ROWS, BLOCK), F32), pltpu.SemaphoreType.DMA((6,))],
         compiler_params=pltpu.CompilerParams(vmem_limit_bytes=SCOPED),
         name="update",
     )(pattern, full, low, up, mat, pivot_rows)

time: 143 us -> 141 us (0.986)
    pallas_call x1, Pallas kernels: 7.54 us -> 5.72 us  [update(): pl.pallas_call(update_kernel, out_shape=jax.ShapeDtypeStruct((ROWS, COLS)...]
where the time goes in v4:
time: 141 us
  Pallas kernels  141 us (100%)
    pallas_call x1, Pallas kernels, exchange(): pl.pallas_call(exchange_kernel, out_shape=(pltpu.VMEM(shape, tiles.dtype)...  86.9 us
    pallas_call x1, Pallas kernels, share(): pl.pallas_call(share_kernel, out_shape=(pltpu.VMEM((ROWS, 2 * PANEL), BF1...  43.8 us
    pallas_call x1, Pallas kernels, update(): pl.pallas_call(update_kernel, out_shape=jax.ShapeDtypeStruct((ROWS, COLS)...  5.72 us
    pallas_call x1, Pallas kernels, assemble(): pl.pallas_call(assemble_kernel, out_shape=pltpu.VMEM((ROWS, COLS), F32),...  4.27 us

profile of v4, /device:TPU:47, one launch (start us, length us, event | category | flops | bytes accessed | tf_op | source)
XLA Modules:
  0.0 140.7 jit_solution(16546024834191479311)
XLA Ops:
  0.0 86.9 %exchange.1 = (bf16[4,4,2,7,128,128]{5,4,3,2,1,0:T(8,128)(2,1)S(1)}, s32[32,1,224]{2,1,0:T(1,128)S(1)}, f32[2048,1024]{1,0:T(8,128)S(1)}, bf16[2,4,4,7,128,128]{5,4,3,2,1,0:T(8,128)(2,1)}) custom-call(bf16[4,4,2,7,128,128]{5,4,3,2,1,0:T(8,128)(2,1)} %bitcast.3, s32[1,224]{1,0:T(1,128)} %own_map.1, f32[2048,1024]{1,0:T(8,128)} %front.1), custom_call_target="tpu_custom_call" | custom-call | tf_op jit(solution)/shard_map/exchange/pallas_call | solution.py:130
  86.9 0.0 copy-start
  86.9 0.0 copy-start.1
  86.9 4.3 %assemble.1.full = f32[2048,1024]{1,0:T(8,128)S(1)} custom-call(s32[32,1,224]{2,1,0:T(1,128)S(1)} %get-tuple-element.12.maps, bf16[224,128,128]{2,1,0:T(8,128)(2,1)S(1)} %bitcast.2, f32[2048,1024]{1,0:T(8,128)S(1)} %get-tuple-element.14.front), custom_call_target="tpu_custom_call", output_to_operand_aliasing={{}: (2, {})} | custom-call | tf_op jit(solution)/shard_map/assemble/pallas_call | solution.py:180
  91.2 0.0 copy-done
  91.2 0.0 copy-done.1
  91.2 43.8 %share.1 = (bf16[2048,1024]{1,0:T(8,128)(2,1)S(1)}, bf16[1024,1024]{1,0:T(8,128)(2,1)S(1)}, f32[2048,1024]{1,0:T(8,128)S(1)}, f32[512,1024]{1,0:T(8,128)S(1)}) custom-call(f32[2048,1024]{1,0:T(8,128)S(1)} %assemble.1.full, f32[2,512,512]{2,1,0:T(8,128)S(1)} %copy-done, s32[64,64]{1,0:T(8,128)S(1)} %copy-done.1), custom_call_target="tpu_custom_call" | custom-call | tf_op jit(solution)/shard_map/share/pallas_call | solution.py:536
  135.0 5.7 %update.1 = f32[2048,1024]{1,0:T(8,128)} custom-call(s32[64,64]{1,0:T(8,128)S(1)} %copy-done.1, f32[2048,1024]{1,0:T(8,128)S(1)} %assemble.1.full, bf16[2048,1024]{1,0:T(8,128)(2,1)S(1)} %get-tuple-element.15.low, bf16[1024,1024]{1,0:T(8,128)(2,1)S(1)} %get-tuple-element.16.up, f32[2048,1024]{1,0:T(8,128)S(1)} %get-tuple-element.17.mat, ...), custom_call_target="tpu_custom_call" | custom-call | tf_op jit(solution)/shard_map/update/pallas_call | solution.py:639
Async XLA Ops:
  86.9 4.3 %copy-start = (f32[2,512,512]{2,1,0:T(8,128)S(1)}, f32[2,512,512]{2,1,0:T(8,128)}, u32[]{:S(2)}) copy-start(f32[2,512,512]{2,1,0:T(8,128)} %inverse.1) | copy-start | bytes 6291460
  86.9 4.3 %copy-start.1 = (s32[64,64]{1,0:T(8,128)S(1)}, s32[64,64]{1,0:T(8,128)}, u32[]{:S(2)}) copy-start(s32[64,64]{1,0:T(8,128)} %pattern.3) | copy-start | bytes 49156

commit v5 on v4

--- a/solution.py
+++ b/solution.py
@@ -191,8 +191,8 @@
 PART = 2
 PIECES = 4 * PART
 WINDOW = 3
-SKEW = 2
-LEAD = 2
+SKEW = 3
+LEAD = 1
 GAP = max(0, 2 * SKEW + LEAD + PART - 1 - PIECES)
 
 UPDATE_AT = PIECES + 3 * SKEW + LEAD
@@ -396,18 +396,6 @@
 
     @pl.loop(0, total + GAP + 3 * SKEW + LEAD)
     def _(t):
-        @pl.when(jnp.logical_not(first_col) & (t >= UPDATE_AT))
-        def _():
-            @pl.when(t == UPDATE_AT)
-            def _():
-                rest_of_first()
-
-            block = t - UPDATE_AT
-
-            @pl.when((block < ROWS // 256) & ((y > 0) | (block >= 4)))
-            def _():
-                first_update(block)
-
         for way in (0, 1):
             j, here = due(t - SKEW * low_hops[way] - LEAD)
 
@@ -491,6 +479,18 @@
                     again(way, g).start()
 
                 paced(core_copy, way, g)
+
+        @pl.when(jnp.logical_not(first_col) & (t >= UPDATE_AT))
+        def _():
+            @pl.when(t == UPDATE_AT)
+            def _():
+                rest_of_first()
+
+            block = t - UPDATE_AT
+
+            @pl.when((block < ROWS // 256) & ((y > 0) | (block >= 4)))
+            def _():
+                first_update(block)
 
     @pl.when(first_row & first_col)
     def _():

time: 141 us -> 141 us (level)
  no operation moved by 1% of the time
where the time goes in v5:
time: 141 us; the launch traced here: 140 us
  Pallas kernels  140 us (99%)
    pallas_call x1, Pallas kernels, exchange(): pl.pallas_call(exchange_kernel, out_shape=(pltpu.VMEM(shape, tiles.dtype)...  86.9 us
    pallas_call x1, Pallas kernels, share(): pl.pallas_call(share_kernel, out_shape=(pltpu.VMEM((ROWS, 2 * PANEL), BF1...  43.6 us
    pallas_call x1, Pallas kernels, update(): pl.pallas_call(update_kernel, out_shape=jax.ShapeDtypeStruct((ROWS, COLS)...  5.71 us
    pallas_call x1, Pallas kernels, assemble(): pl.pallas_call(assemble_kernel, out_shape=pltpu.VMEM((ROWS, COLS), F32),...  4.24 us

profile of v5, /device:TPU:47, one launch (start us, length us, event | category | flops | bytes accessed | tf_op | source)
XLA Modules:
  0.0 140.5 jit_solution(1833398290824485810)
XLA Ops:
  0.0 86.9 %exchange.1 = (bf16[4,4,2,7,128,128]{5,4,3,2,1,0:T(8,128)(2,1)S(1)}, s32[32,1,224]{2,1,0:T(1,128)S(1)}, f32[2048,1024]{1,0:T(8,128)S(1)}, bf16[2,4,4,7,128,128]{5,4,3,2,1,0:T(8,128)(2,1)}) custom-call(bf16[4,4,2,7,128,128]{5,4,3,2,1,0:T(8,128)(2,1)} %bitcast.3, s32[1,224]{1,0:T(1,128)} %own_map.1, f32[2048,1024]{1,0:T(8,128)} %front.1), custom_call_target="tpu_custom_call" | custom-call | tf_op jit(solution)/shard_map/exchange/pallas_call | solution.py:130
  86.9 0.0 copy-start
  86.9 0.0 copy-start.1
  86.9 4.2 %assemble.1.full = f32[2048,1024]{1,0:T(8,128)S(1)} custom-call(s32[32,1,224]{2,1,0:T(1,128)S(1)} %get-tuple-element.12.maps, bf16[224,128,128]{2,1,0:T(8,128)(2,1)S(1)} %bitcast.2, f32[2048,1024]{1,0:T(8,128)S(1)} %get-tuple-element.14.front), custom_call_target="tpu_custom_call", output_to_operand_aliasing={{}: (2, {})} | custom-call | tf_op jit(solution)/shard_map/assemble/pallas_call | solution.py:180
  91.2 0.0 copy-done
  91.2 0.0 copy-done.1
  91.2 43.6 %share.1 = (bf16[2048,1024]{1,0:T(8,128)(2,1)S(1)}, bf16[1024,1024]{1,0:T(8,128)(2,1)S(1)}, f32[2048,1024]{1,0:T(8,128)S(1)}, f32[512,1024]{1,0:T(8,128)S(1)}) custom-call(f32[2048,1024]{1,0:T(8,128)S(1)} %assemble.1.full, f32[2,512,512]{2,1,0:T(8,128)S(1)} %copy-done, s32[64,64]{1,0:T(8,128)S(1)} %copy-done.1), custom_call_target="tpu_custom_call" | custom-call | tf_op jit(solution)/shard_map/share/pallas_call | solution.py:536
  134.8 5.7 %update.1 = f32[2048,1024]{1,0:T(8,128)} custom-call(s32[64,64]{1,0:T(8,128)S(1)} %copy-done.1, f32[2048,1024]{1,0:T(8,128)S(1)} %assemble.1.full, bf16[2048,1024]{1,0:T(8,128)(2,1)S(1)} %get-tuple-element.15.low, bf16[1024,1024]{1,0:T(8,128)(2,1)S(1)} %get-tuple-element.16.up, f32[2048,1024]{1,0:T(8,128)S(1)} %get-tuple-element.17.mat, ...), custom_call_target="tpu_custom_call" | custom-call | tf_op jit(solution)/shard_map/update/pallas_call | solution.py:639
Async XLA Ops:
  86.9 4.3 %copy-start = (f32[2,512,512]{2,1,0:T(8,128)S(1)}, f32[2,512,512]{2,1,0:T(8,128)}, u32[]{:S(2)}) copy-start(f32[2,512,512]{2,1,0:T(8,128)} %inverse.1) | copy-start | bytes 6291460
  86.9 4.3 %copy-start.1 = (s32[64,64]{1,0:T(8,128)S(1)}, s32[64,64]{1,0:T(8,128)}, u32[]{:S(2)}) copy-start(s32[64,64]{1,0:T(8,128)} %pattern.3) | copy-start | bytes 49156

commit v6 on v5

--- a/solution.py
+++ b/solution.py
@@ -562,7 +562,7 @@
     )(full, inverse, pattern)
 
 
-BLOCK = 256
+BLOCK = 512
 HALF = ROWS // 2
 
 
@@ -623,7 +623,7 @@
                             slots[slot, here, part] = mat[here, place] - cut[tile, part] * keep
                     store(block, half).start()
 
-        for block in (2, 3):
+        for block in (0, 1):
             for half in (0, 1):
                 @pl.when((row > 0) | (half == 1))
                 def _(block=block, half=half):

time: 141 us -> 140 us (level)
  no operation moved by 1% of the time
where the time goes in v6:
time: 140 us
  Pallas kernels  140 us (100%)
    pallas_call x1, Pallas kernels, exchange(): pl.pallas_call(exchange_kernel, out_shape=(pltpu.VMEM(shape, tiles.dtype)...  86.9 us
    pallas_call x1, Pallas kernels, share(): pl.pallas_call(share_kernel, out_shape=(pltpu.VMEM((ROWS, 2 * PANEL), BF1...  43.6 us
    pallas_call x1, Pallas kernels, update(): pl.pallas_call(update_kernel, out_shape=jax.ShapeDtypeStruct((ROWS, COLS)...  5.44 us
    pallas_call x1, Pallas kernels, assemble(): pl.pallas_call(assemble_kernel, out_shape=pltpu.VMEM((ROWS, COLS), F32),...  4.27 us

profile of v6, /device:TPU:47, one launch (start us, length us, event | category | flops | bytes accessed | tf_op | source)
XLA Modules:
  0.0 140.2 jit_solution(5450121934897366908)
XLA Ops:
  0.0 86.9 %exchange.1 = (bf16[4,4,2,7,128,128]{5,4,3,2,1,0:T(8,128)(2,1)S(1)}, s32[32,1,224]{2,1,0:T(1,128)S(1)}, f32[2048,1024]{1,0:T(8,128)S(1)}, bf16[2,4,4,7,128,128]{5,4,3,2,1,0:T(8,128)(2,1)}) custom-call(bf16[4,4,2,7,128,128]{5,4,3,2,1,0:T(8,128)(2,1)} %bitcast.3, s32[1,224]{1,0:T(1,128)} %own_map.1, f32[2048,1024]{1,0:T(8,128)} %front.1), custom_call_target="tpu_custom_call" | custom-call | tf_op jit(solution)/shard_map/exchange/pallas_call | solution.py:130
  86.9 0.0 copy-start
  86.9 0.0 copy-start.1
  86.9 4.3 %assemble.1.full = f32[2048,1024]{1,0:T(8,128)S(1)} custom-call(s32[32,1,224]{2,1,0:T(1,128)S(1)} %get-tuple-element.12.maps, bf16[224,128,128]{2,1,0:T(8,128)(2,1)S(1)} %bitcast.2, f32[2048,1024]{1,0:T(8,128)S(1)} %get-tuple-element.14.front), custom_call_target="tpu_custom_call", output_to_operand_aliasing={{}: (2, {})} | custom-call | tf_op jit(solution)/shard_map/assemble/pallas_call | solution.py:180
  91.2 0.0 copy-done
  91.2 0.0 copy-done.1
  91.2 43.6 %share.1 = (bf16[2048,1024]{1,0:T(8,128)(2,1)S(1)}, bf16[1024,1024]{1,0:T(8,128)(2,1)S(1)}, f32[2048,1024]{1,0:T(8,128)S(1)}, f32[512,1024]{1,0:T(8,128)S(1)}) custom-call(f32[2048,1024]{1,0:T(8,128)S(1)} %assemble.1.full, f32[2,512,512]{2,1,0:T(8,128)S(1)} %copy-done, s32[64,64]{1,0:T(8,128)S(1)} %copy-done.1), custom_call_target="tpu_custom_call" | custom-call | tf_op jit(solution)/shard_map/share/pallas_call | solution.py:536
  134.8 5.4 %update.1 = f32[2048,1024]{1,0:T(8,128)} custom-call(s32[64,64]{1,0:T(8,128)S(1)} %copy-done.1, f32[2048,1024]{1,0:T(8,128)S(1)} %assemble.1.full, bf16[2048,1024]{1,0:T(8,128)(2,1)S(1)} %get-tuple-element.15.low, bf16[1024,1024]{1,0:T(8,128)(2,1)S(1)} %get-tuple-element.16.up, f32[2048,1024]{1,0:T(8,128)S(1)} %get-tuple-element.17.mat, ...), custom_call_target="tpu_custom_call" | custom-call | tf_op jit(solution)/shard_map/update/pallas_call | solution.py:639
Async XLA Ops:
  86.9 4.3 %copy-start = (f32[2,512,512]{2,1,0:T(8,128)S(1)}, f32[2,512,512]{2,1,0:T(8,128)}, u32[]{:S(2)}) copy-start(f32[2,512,512]{2,1,0:T(8,128)} %inverse.1) | copy-start | bytes 6291460
  86.9 4.3 %copy-start.1 = (s32[64,64]{1,0:T(8,128)S(1)}, s32[64,64]{1,0:T(8,128)}, u32[]{:S(2)}) copy-start(s32[64,64]{1,0:T(8,128)} %pattern.3) | copy-start | bytes 49156
